TPU v7x, 32 devices: a whole 2x2x4 slice. The times are simulated.
32 devices in a mesh: track: 2 (over y), tm: 16 (over z, x, core).
Axes of the slice: x: 2, y: 2, z: 4, core: 2. Of those that a mesh axis runs over, the one named last changes fastest.
Arguments:
- track_query: bfloat16 [16, 2048, 1024], P('track', 'tm'), may hold values from -6 to 6
- track_key: bfloat16 [16, 2048, 1024], P('track', 'tm'), may hold values from -6 to 6
- track_value: bfloat16 [16, 2048, 1024], P('track', 'tm'), may hold values from -6 to 6
- log_decay: float32 [16, 8, 2048], P('track', None, 'tm'), may hold values from -2.3 to 0
- valid_length: int32 [16], replicated, may hold values from 512 to 2048, as said below
- initial_state: bfloat16 [16, 8, 128, 128], P('track'), may hold values from -24 to 24
- cross_query: bfloat16 [16, 2048, 1024], P('track', 'tm'), may hold values from -5 to 5
- cross_key: bfloat16 [16, 2048, 1024], P('track', 'tm'), may hold values from -5 to 5
- grad_out: bfloat16 [16, 2048, 1024], P('track', 'tm'), may hold values from -6 to 6
Outputs:
- grad_query: bfloat16 [16, 2048, 1024], P('track', 'tm')
- grad_key: bfloat16 [16, 2048, 1024], P('track', 'tm')
- grad_value: bfloat16 [16, 2048, 1024], P('track', 'tm')
- grad_cross_query: bfloat16 [16, 2048, 1024], P('track', 'tm')
- grad_cross_key: bfloat16 [16, 2048, 1024], P('track', 'tm')
Inputs may be any that keep to these rules, and one draw needn't show every extreme that they name: `valid_length`: multiples of 128; one track has 2048 valid steps and one has exactly 512.
All inputs are finite; a program needn't handle non-finite values.
Results may differ from a plain program's by a relative error of at most 0.005.
Values may be sent and summed in bfloat16 or wider, within the bound.
A program may use at most 256 MiB of HBM per device.

v0:
```python
import jax
import jax.numpy as jnp
from jax import lax
from jax.sharding import PartitionSpec as P

EPSILON = 1e-06
HIGHEST_PRECISION = lax.Precision.HIGHEST


def prefix_2(value, axis, join, neutral, backward):
    count, mine = (lax.axis_size(axis), lax.axis_index(axis))
    pieces = jax.tree.map(lambda part: lax.all_gather(part, axis), value)
    if backward:
        pieces = jax.tree.map(lambda part: part[::-1], pieces)
        mine = count - 1 - mine
    running = jax.tree.map(
        lambda part, zero: jnp.full_like(part, 0) + jnp.asarray(zero, part.dtype), value, neutral
    )

    def lap(position, running):
        longer = join(running, jax.tree.map(lambda part: part[position], pieces))
        return jax.tree.map(lambda new, old: jnp.where(position < mine, new, old), longer, running)

    return lax.fori_loop(0, count - 1, lap, running)


def carry_combine(earlier, later):
    return (earlier[0] * later[0], later[0][:, :, None, None] * earlier[1] + later[1])


def per_device(
    track_query,
    track_key,
    track_value,
    log_decay,
    valid_length,
    initial_state,
    cross_query,
    cross_key,
    grad_out,
):
    local_tracks, local_time, model_width = track_query.shape
    head_count = log_decay.shape[1]
    head_size = model_width // head_count
    block_rows = min(128, local_time)
    blocks = local_time // block_rows
    group_size = lax.axis_size("track")
    all_tracks = valid_length.shape[0]
    time_first = lax.axis_index("tm") * local_time
    track_ids = lax.axis_index("track") * local_tracks + jnp.arange(local_tracks)
    picked = jnp.arange(all_tracks)[None, :] == track_ids[:, None]
    own_length = jnp.sum(jnp.where(picked, valid_length[None, :], 0), axis=1)
    time_index = time_first + jnp.arange(local_time)
    valid_rows = (time_index[None, :] < own_length[:, None]).astype(jnp.float32)
    five_dims = (local_tracks, blocks, block_rows, head_count, head_size)
    query_blocks = track_query.reshape(five_dims)
    key_masked = (track_key * valid_rows[:, :, None].astype(jnp.bfloat16)).reshape(five_dims)
    value_blocks = track_value.reshape(five_dims)
    query_float = query_blocks.astype(jnp.float32)
    key_float = key_masked.astype(jnp.float32)
    value_float = value_blocks.astype(jnp.float32)
    mask_rows = valid_rows.reshape(local_tracks, blocks, block_rows)[..., None, None]
    within = jnp.cumsum(log_decay.reshape(local_tracks, head_count, blocks, block_rows), axis=-1)
    lower_mask = jnp.arange(block_rows)[:, None] >= jnp.arange(block_rows)[None, :]
    decay_matrix = jnp.exp(
        jnp.where(lower_mask, within[..., :, None] - within[..., None, :], -jnp.inf)
    )
    to_end_rows = jnp.transpose(jnp.exp(within[..., -1:] - within), (0, 2, 3, 1))[..., None]
    from_start_rows = jnp.transpose(jnp.exp(within), (0, 2, 3, 1))[..., None]
    block_decay = jnp.exp(within[..., -1])
    device_decay = jnp.exp(jnp.sum(log_decay, axis=-1))
    scores = (
        jnp.einsum(
            "xnthc,xnshc->xhnts", query_blocks, key_masked, preferred_element_type=jnp.float32
        )
        * decay_matrix
    )
    intra_out = jnp.einsum("xhnts,xnshd->xnthd", scores, value_float, precision=HIGHEST_PRECISION)
    block_states = jnp.einsum(
        "xnshc,xnshd->xhncd", key_float * to_end_rows, value_float, precision=HIGHEST_PRECISION
    )
    zero_state = jnp.zeros((local_tracks, head_count, head_size, head_size), jnp.float32)
    partial_value = [zero_state]
    lead_in = [jnp.ones_like(device_decay)]
    position = 0
    partial_value.append(
        block_decay[:, :, position, None, None] * partial_value[-1] + block_states[:, :, position]
    )
    lead_in.append(lead_in[-1] * block_decay[:, :, position])
    prefix = prefix_2(
        (device_decay, partial_value[-1]),
        "tm",
        carry_combine,
        (jnp.ones_like(device_decay), jnp.zeros_like(zero_state)),
        False,
    )
    state_in = prefix[1] + prefix[0][:, :, None, None] * initial_state.astype(jnp.float32)
    start_states = jnp.stack([partial_value[0] + lead_in[0][:, :, None, None] * state_in], axis=2)
    outputs = intra_out + from_start_rows * jnp.einsum(
        "xnthc,xhncd->xnthd", query_float, start_states, precision=HIGHEST_PRECISION
    )
    mean_square = jnp.mean(outputs * outputs, axis=-1, keepdims=True)
    inverse = 1.0 / jnp.sqrt(mean_square + EPSILON)
    four_dims = (local_tracks, local_time, head_count, head_size)
    normed = (outputs * inverse * mask_rows).astype(jnp.bfloat16).reshape(four_dims)
    query_cross = cross_query.reshape(four_dims)
    key_cross = cross_key.reshape(four_dims)
    grad_rows = grad_out.reshape(four_dims)
    normed_x, query_x, key_x, grad_x = (
        lax.all_to_all(normed, "track", split_axis=1, concat_axis=0, tiled=True),
        lax.all_to_all(query_cross, "track", split_axis=1, concat_axis=0, tiled=True),
        lax.all_to_all(key_cross, "track", split_axis=1, concat_axis=0, tiled=True),
        lax.all_to_all(grad_rows, "track", split_axis=1, concat_axis=0, tiled=True),
    )
    time_rows = local_time // group_size
    block_times = time_first + lax.axis_index("track") * time_rows + jnp.arange(time_rows)
    key_valid = block_times[None, :] < valid_length[:, None]
    scale_root = float(head_size) ** 0.5
    logits = (
        jnp.einsum("irhc,jrhc->rhij", query_x, key_x, preferred_element_type=jnp.float32)
        / scale_root
    )
    logits = jnp.where(jnp.transpose(key_valid)[:, None, None, :], logits, -1e30)
    row_max = jnp.max(logits, axis=-1, keepdims=True)
    weights = jnp.exp(logits - row_max)
    weights = weights / jnp.sum(weights, axis=-1, keepdims=True)
    grad_masked_half = grad_x * key_valid.astype(jnp.bfloat16)[:, :, None, None]
    grad_masked = grad_masked_half.astype(jnp.float32)
    grad_weights = jnp.einsum(
        "irhc,jrhc->rhij", grad_masked_half, normed_x, preferred_element_type=jnp.float32
    )
    grad_logits = (
        weights
        * (grad_weights - jnp.sum(weights * grad_weights, axis=-1, keepdims=True))
        / scale_root
    )
    grad_normed = jnp.einsum(
        "rhij,irhc->jrhc", weights, grad_masked, precision=HIGHEST_PRECISION
    ).astype(jnp.bfloat16)
    grad_query_x = jnp.einsum(
        "rhij,jrhc->irhc", grad_logits, key_x.astype(jnp.float32), precision=HIGHEST_PRECISION
    ).astype(jnp.bfloat16)
    grad_key_x = jnp.einsum(
        "rhij,irhc->jrhc", grad_logits, query_x.astype(jnp.float32), precision=HIGHEST_PRECISION
    ).astype(jnp.bfloat16)
    grad_normed_t, grad_query_t, grad_key_t = (
        lax.all_to_all(grad_normed, "track", split_axis=0, concat_axis=1, tiled=True),
        lax.all_to_all(grad_query_x, "track", split_axis=0, concat_axis=1, tiled=True),
        lax.all_to_all(grad_key_x, "track", split_axis=0, concat_axis=1, tiled=True),
    )
    grad_unit = grad_normed_t.astype(jnp.float32).reshape(five_dims)
    along_output = jnp.sum(grad_unit * outputs, axis=-1, keepdims=True)
    grad_outputs = mask_rows * (
        inverse * grad_unit - inverse * inverse * inverse / head_size * along_output * outputs
    )
    grad_scores = (
        jnp.einsum("xnthd,xnshd->xhnts", grad_outputs, value_float, precision=HIGHEST_PRECISION)
        * decay_matrix
    )
    to_state = jnp.einsum(
        "xnthc,xnthd->xhncd",
        query_float * from_start_rows,
        grad_outputs,
        precision=HIGHEST_PRECISION,
    )
    local_grad = [zero_state]
    position = 0
    local_grad.insert(
        0, to_state[:, :, position] + block_decay[:, :, position, None, None] * local_grad[0]
    )
    tail_decay = jnp.ones_like(device_decay)
    end_grad = prefix_2(
        (device_decay, local_grad[0]),
        "tm",
        carry_combine,
        (jnp.ones_like(device_decay), jnp.zeros_like(zero_state)),
        True,
    )[1]
    out_grads = jnp.stack([local_grad[1] + tail_decay[:, :, None, None] * end_grad], axis=2)
    grad_query = jnp.einsum(
        "xhnts,xnshc->xnthc", grad_scores, key_float, precision=HIGHEST_PRECISION
    )
    grad_query = grad_query + from_start_rows * jnp.einsum(
        "xnthd,xhncd->xnthc", grad_outputs, start_states, precision=HIGHEST_PRECISION
    )
    grad_key = jnp.einsum(
        "xhnts,xnthc->xnshc", grad_scores, query_float, precision=HIGHEST_PRECISION
    )
    grad_key = (
        grad_key
        + to_end_rows
        * jnp.einsum("xnshd,xhncd->xnshc", value_float, out_grads, precision=HIGHEST_PRECISION)
    ) * mask_rows
    grad_value = jnp.einsum("xhnts,xnthd->xnshd", scores, grad_outputs, precision=HIGHEST_PRECISION)
    grad_value = grad_value + to_end_rows * jnp.einsum(
        "xnshc,xhncd->xnshd", key_float, out_grads, precision=HIGHEST_PRECISION
    )
    flat_shape = (local_tracks, local_time, model_width)
    return (
        grad_query.astype(jnp.bfloat16).reshape(flat_shape),
        grad_key.astype(jnp.bfloat16).reshape(flat_shape),
        grad_value.astype(jnp.bfloat16).reshape(flat_shape),
        grad_query_t.reshape(flat_shape),
        grad_key_t.reshape(flat_shape),
    )


def solution(mesh):
    placed = (
        P("track", "tm", None),
        P("track", "tm", None),
        P("track", "tm", None),
        P("track", None, "tm"),
        P(),
        P("track", None, None, None),
        P("track", "tm", None),
        P("track", "tm", None),
        P("track", "tm", None),
    )
    return jax.shard_map(
        per_device,
        mesh=mesh,
        in_specs=placed,
        out_specs=(
            P("track", "tm", None),
            P("track", "tm", None),
            P("track", "tm", None),
            P("track", "tm", None),
            P("track", "tm", None),
        ),
        check_vma=False,
    )
```

profile of v0, /device:TPU:0, one launch (start us, length us, event | category | flops | bytes accessed | tf_op | source)
XLA Modules:
  0.0 959.8 jit_solution(14730933613541237104)
XLA Ops:
  40.4 21.7 %all-to-all-done.1 = bf16[8,128,8,128]{3,2,0,1:T(8,128)(2,1)} async-done(((bf16[8,128,8,128]{3,2,0,1:T(8,128)(2,1)}), bf16[8,128,8,128]{3,2,0,1:T(8,128)(2,1)}, u32[]{:S(2)}, u32[]{:S(2)}) %all-to-all-start.1) | async-done | bytes 2097184 | tf_op jit(solution)/shard_map/all_to_all | solution.py:111
  71.3 20.3 %all-to-all-done.2 = bf16[8,128,8,128]{3,2,0,1:T(8,128)(2,1)} async-done(((bf16[8,128,8,128]{3,2,0,1:T(8,128)(2,1)}), bf16[8,128,8,128]{3,2,0,1:T(8,128)(2,1)}, u32[]{:S(2)}, u32[]{:S(2)}) %all-to-all-start.2) | async-done | bytes 2097184 | tf_op jit(solution)/shard_map/all_to_all | solution.py:112
  104.3 16.1 %all-to-all-done = bf16[8,128,8,128]{3,2,0,1:T(8,128)(2,1)} async-done(((bf16[8,128,8,128]{3,2,0,1:T(8,128)(2,1)}), bf16[8,128,8,128]{3,2,0,1:T(8,128)(2,1)}, u32[]{:S(2)}, u32[]{:S(2)}) %all-to-all-start) | async-done | bytes 2097184 | tf_op jit(solution)/shard_map/all_to_all | solution.py:113
  120.4 6.5 convert_bitcast_fusion.3
  137.7 22.2 %all-gather = f32[128,8]{1,0:T(8,128)S(1)} all-gather(f32[8,8]{1,0:T(8,128)S(1)} %exp.50), channel_id=2, replica_groups=mesh['track'=2,'tm'=16] {'tm'}, dimensions={0}, use_global_device_ids=true | all-gather | bytes 4352 | tf_op jit(solution)/shard_map/all_gather | solution.py:12
  180.2 175.6 %all-gather.6.cloned.1.call-done = f32[128,8,128,128]{3,2,1,0:T(8,128)} async-done(((f32[8,8,128,128]{3,2,1,0:T(8,128)}), f32[128,8,128,128]{3,2,1,0:T(8,128)}) %all-gather.6.cloned.1.call-update) | async-done | bytes 67108880 | tf_op jit(solution)/shard_map/all_gather | solution.py:12
  355.9 89.4 %while.30 = (s32[]{:T(128)}, f32[8,8]{1,0:T(8,128)S(1)}, f32[8,8,128,128]{3,2,1,0:T(8,128)}, s32[]{:T(128)}, f32[16,8,8]{2,1,0:T(8,128)S(1)}, /*index=5*/f32[16,8,8,128,128]{4,3,2,1,0:T(8,128)}, s32[]{:T(128)}, s32[]{:T(128)}) while((s32[]{:T(128)}, f32[8,8]{1,0:T(8,128)S(1)}, f32[8,8,128,128]{3,2,1,0:T(8,128)}, s32[]{:T(128)}, ...), condition=%wide.region_4.5_spmd.clone, body=%wide.region_3.4_spmd.clone.sunk | while | flops 4194500 | bytes 12584315 | solution.py:24
  445.2 9.9 %multiply_reduce_fusion.2 = (f32[8,128,8]{1,2,0:T(8,128)S(1)}, f32[8,128,8]{1,2,0:T(8,128)S(1)}, f32[8,1,128,8,128]{2,4,3,0,1:T(8,128)S(1)}) fusion(f32[8,1,128,8,128]{2,4,3,0,1:T(8,128)} %copy.240, bf16[8,128,8,128]{1,3,2,0:T(8,128)(2,1)} %bitcast.225, f32[8,8,128,128]{3,2,1,0:T(8,128)} %get-tuple-element.209, bf16[8,8,128,128]{3,2,1,0:T(8,128)(2,1)} %param.18, ...), kind=kOutput, calls=%fused_computation.38 | convolution fusion | flops 1620033536 | bytes 21070080 | tf_op jit(solution)/shard_map/xnthc,xhncd->xnthd/dot_general | solution.py:99
  460.0 10.1 %fusion.33 = f32[8,8,128,128]{3,2,1,0:T(8,128)} fusion(f32[8,1,128,8,128]{2,4,3,0,1:T(8,128)S(1)} %get-tuple-element.310, bf16[8,128,8,128]{1,3,2,0:T(8,128)(2,1)S(1)} %bitcast.227, f32[8,128,8]{1,2,0:T(8,128)S(1)} %get-tuple-element.313, f32[8,8]{1,0:T(8,128)S(1)} %get-tuple-element.283), kind=kOutput, calls=%fused_computation.52 | convolution fusion | flops 1613758464 | bytes 10518784 | tf_op jit(solution)/shard_map/xnthc,xnthd->xhncd/dot_general | solution.py:160
  479.5 11.3 %fusion.14 = f32[8,8,128,128]{3,2,1,0:T(8,128)} fusion(f32[8,1,128,8,128]{2,4,3,0,1:T(8,128)} %copy-done.2, f32[8,8,128,128]{3,2,1,0:T(8,128)} %get-tuple-element.209, bf16[8,8,128,128]{3,2,1,0:T(8,128)(2,1)} %param.18, f32[8,8]{1,0:T(8,128)S(1)} %get-tuple-element.210), kind=kOutput, calls=%fused_computation.24 | convolution fusion | flops 1613758464 | bytes 14680320 | tf_op jit(solution)/shard_map/xnthd,xhncd->xnthc/dot_general | solution.py:183
  490.8 14.2 %all-to-all-done.4 = bf16[8,128,8,128]{3,2,0,1:T(8,128)(2,1)} async-done(((bf16[8,128,8,128]{3,2,0,1:T(8,128)(2,1)}), bf16[8,128,8,128]{3,2,0,1:T(8,128)(2,1)}, u32[]{:S(2)}, u32[]{:S(2)}) %all-to-all-start.4) | async-done | bytes 2097184 | tf_op jit(solution)/shard_map/all_to_all | solution.py:110
  505.0 6.7 multiply_reduce_fusion
  511.7 6.3 convert_bitcast_fusion.1
  525.0 7.0 fusion.16
  532.0 6.5 convert_bitcast_fusion.2
  540.4 9.2 all-to-all-done.6
  554.5 9.2 fusion.8
  567.9 10.0 %fusion.25 = f32[8,8,128,128]{2,3,1,0:T(8,128)} fusion(bf16[8,128,8,128]{1,3,2,0:T(8,128)(2,1)} %bitcast.226, f32[8,8,128,128]{2,3,1,0:T(8,128)} %fusion.16, f32[8,8,128]{2,1,0:T(8,128)S(1)} %bitcast.239, pred[128,128]{0,1:T(8,128)(4,1)S(1)} %iota_compare_fusion), kind=kOutput, calls=%fused_computation.46 | convolution fusion | flops 1613758464 | bytes 10534912 | tf_op jit(solution)/shard_map/xhnts,xnthc->xnshc/dot_general | solution.py:186
  577.8 10.6 %fusion.10 = f32[8,8,128,128]{3,2,1,0:T(8,128)} fusion(f32[8,1,128,8,128]{2,4,3,0,1:T(8,128)S(1)} %copy-done.3, f32[8,8,128,128]{3,2,1,0:T(8,128)S(1)} %copy-done.6, f32[8,8,128]{2,1,0:T(8,128)S(1)} %bitcast.240, pred[128,128]{0,1:T(8,128)(4,1)S(1)} %iota_compare_fusion), kind=kOutput, calls=%fused_computation.20 | convolution fusion | flops 1613758464 | bytes 12632064 | tf_op jit(solution)/shard_map/xhnts,xnthd->xnshd/dot_general | solution.py:194
  603.0 193.8 %all-gather.8.cloned.1.call-done = f32[128,8,128,128]{3,2,1,0:T(8,128)} async-done(((f32[8,8,128,128]{3,2,1,0:T(8,128)}), f32[128,8,128,128]{3,2,1,0:T(8,128)}) %all-gather.8.cloned.1.call-update) | async-done | bytes 67108880 | tf_op jit(solution)/shard_map/all_gather | solution.py:12
  796.8 43.8 %rev.7 = f32[16,8,8,128,128]{4,3,2,1,0:T(8,128)} reverse(f32[16,8,8,128,128]{4,3,2,1,0:T(8,128)} %bitcast.41), dimensions={0} | reverse | bytes 134217728 | tf_op jit(solution)/shard_map/rev | solution.py:14
  840.6 89.7 %while.31 = (s32[]{:T(128)}, f32[8,8,128,128]{3,2,1,0:T(8,128)}, s32[]{:T(128)}, f32[16,8,8]{2,1,0:T(8,128)S(1)}, f32[16,8,8,128,128]{4,3,2,1,0:T(8,128)}, /*index=5*/s32[]{:T(128)}, s32[]{:T(128)}) while((s32[]{:T(128)}, f32[8,8,128,128]{3,2,1,0:T(8,128)}, s32[]{:T(128)}, f32[16,8,8]{2,1,0:T(8,128)S(1)}, ...), condition=%wide.region_10.11_spmd.clone, body=%wide.region_9.10_spmd.clone.sunk | while | flops 4194308 | bytes 12583793 | solution.py:24
  845.4 6.0 fusion.127
  851.5 6.0 fusion.127
  857.5 6.0 fusion.127
  863.6 6.0 fusion.127
  893.8 6.0 fusion.127
  899.8 6.0 fusion.127
  905.9 6.0 fusion.127
  911.9 6.0 fusion.127
  918.0 6.0 fusion.127
  930.4 9.4 fusion.6
  (156 shorter events, 269.8 us)
Async XLA Ops:
  7.2 13.4 %copy-start = (bf16[8,128,1024]{2,1,0:T(8,128)(2,1)S(1)}, bf16[8,128,1024]{2,1,0:T(8,128)(2,1)}, u32[]{:S(2)}) copy-start(bf16[8,128,1024]{2,1,0:T(8,128)(2,1)} %param.15) | copy-start | bytes 6291460
  7.2 348.7 %all-gather.6.cloned.1.call-start = ((), (), s32[]{:S(2)}) async-start(), calls=%async_computation.7 | async-start | bytes 71303168 | tf_op jit(solution)/shard_map/all_gather | solution.py:12
  11.8 8.8 copy-start.13
  12.7 147.3 %copy-start.16 = (bf16[8,128]{1,0:T(8,128)(2,1)}, bf16[8,128]{1,0:T(8,128)(2,1)S(1)}, u32[]{:S(2)}) copy-start(bf16[8,128]{1,0:T(8,128)(2,1)S(1)} %get-tuple-element.316) | copy-start | bytes 6148
  30.8 31.3 %all-to-all-start.1 = ((bf16[8,128,8,128]{3,2,0,1:T(8,128)(2,1)}), bf16[8,128,8,128]{3,2,0,1:T(8,128)(2,1)}, u32[]{:S(2)}, u32[]{:S(2)}) async-start(bf16[8,128,8,128]{3,2,0,1:T(8,128)(2,1)} %copy.279), calls=%async_computation.1 | async-start | bytes 4194304 | tf_op jit(solution)/shard_map/all_to_all | solution.py:111
  38.4 28.6 %copy-start.18 = (s32[16]{0:T(128)S(1)}, s32[16]{0:T(128)}, u32[]{:S(2)}) copy-start(s32[16]{0:T(128)} %param.17) | copy-start | bytes 196
  62.1 29.5 %all-to-all-start.2 = ((bf16[8,128,8,128]{3,2,0,1:T(8,128)(2,1)}), bf16[8,128,8,128]{3,2,0,1:T(8,128)(2,1)}, u32[]{:S(2)}, u32[]{:S(2)}) async-start(bf16[8,128,8,128]{3,2,0,1:T(8,128)(2,1)} %copy.281), calls=%async_computation.2 | async-start | bytes 4194304 | tf_op jit(solution)/shard_map/all_to_all | solution.py:112
  91.6 28.8 %all-to-all-start = ((bf16[8,128,8,128]{3,2,0,1:T(8,128)(2,1)}), bf16[8,128,8,128]{3,2,0,1:T(8,128)(2,1)}, u32[]{:S(2)}, u32[]{:S(2)}) async-start(bf16[8,128,8,128]{3,2,0,1:T(8,128)(2,1)} %copy.278), calls=%async_computation | async-start | bytes 4194304 | tf_op jit(solution)/shard_map/all_to_all | solution.py:113
  100.6 2.0 copy-start.10
  126.9 6.8 copy-start.15
  128.8 41.7 %all-to-all-start.3 = ((bf16[16,64,8,128]{3,2,1,0:T(8,128)(2,1)}), bf16[16,64,8,128]{3,2,1,0:T(8,128)(2,1)}, u32[]{:S(2)}, u32[]{:S(2)}) async-start(bf16[16,64,8,128]{3,2,1,0:T(8,128)(2,1)} %copy.238), calls=%async_computation.3 | async-start | bytes 4194304 | tf_op jit(solution)/shard_map/all_to_all | solution.py:147
  133.6 663.1 %all-gather.8.cloned.1.call-start = ((), (), s32[]{:S(2)}) async-start(), calls=%async_computation.8 | async-start | bytes 71303168 | tf_op jit(solution)/shard_map/all_gather | solution.py:12
  163.0 2.0 copy-start.5
  445.2 9.9 %copy-start.7 = (f32[8,1,128,8,128]{2,4,3,0,1:T(8,128)S(1)}, f32[8,1,128,8,128]{2,4,3,0,1:T(8,128)}, u32[]{:S(2)}) copy-start(f32[8,1,128,8,128]{2,4,3,0,1:T(8,128)} %copy.240) | copy-start | bytes 12582916
  455.1 4.9 copy-start.4
  458.0 2.0 copy-start.2
  474.3 30.7 %all-to-all-start.4 = ((bf16[8,128,8,128]{3,2,0,1:T(8,128)(2,1)}), bf16[8,128,8,128]{3,2,0,1:T(8,128)(2,1)}, u32[]{:S(2)}, u32[]{:S(2)}) async-start(bf16[8,128,8,128]{3,2,0,1:T(8,128)(2,1)} %copy.256), calls=%async_computation.4 | async-start | bytes 4194304 | tf_op jit(solution)/shard_map/all_to_all | solution.py:110
  505.0 6.7 copy-start.11
  511.7 6.4 copy-start.19
  519.9 29.7 %all-to-all-start.6 = ((bf16[16,64,8,128]{3,2,1,0:T(8,128)(2,1)}), bf16[16,64,8,128]{3,2,1,0:T(8,128)(2,1)}, u32[]{:S(2)}, u32[]{:S(2)}) async-start(bf16[16,64,8,128]{3,2,1,0:T(8,128)(2,1)} %copy.262), calls=%async_computation.6 | async-start | bytes 4194304 | tf_op jit(solution)/shard_map/all_to_all | solution.py:149
  525.0 7.0 copy-start.12
  525.0 7.0 copy-start.20
  549.6 46.0 %all-to-all-start.5 = ((bf16[16,64,8,128]{3,2,1,0:T(8,128)(2,1)}), bf16[16,64,8,128]{3,2,1,0:T(8,128)(2,1)}, u32[]{:S(2)}, u32[]{:S(2)}) async-start(bf16[16,64,8,128]{3,2,1,0:T(8,128)(2,1)} %copy.260), calls=%async_computation.5 | async-start | bytes 4194304 | tf_op jit(solution)/shard_map/all_to_all | solution.py:148
  567.9 10.0 %copy-start.3 = (f32[8,1,128,8,128]{2,4,3,0,1:T(8,128)S(1)}, f32[8,1,128,8,128]{2,4,3,0,1:T(8,128)}, u32[]{:S(2)}) copy-start(f32[8,1,128,8,128]{2,4,3,0,1:T(8,128)} %copy-done.2) | copy-start | bytes 12582916
  567.9 10.0 %copy-start.6 = (f32[8,8,128,128]{3,2,1,0:T(8,128)S(1)}, f32[8,8,128,128]{3,2,1,0:T(8,128)}, u32[]{:S(2)}) copy-start(f32[8,8,128,128]{3,2,1,0:T(8,128)} %copy-done.5) | copy-start | bytes 12582916
  840.6 89.7 %copy-start.14 = (f32[8,128,8]{1,2,0:T(8,128)S(1)}, f32[8,128,8]{1,2,0:T(8,128)}, u32[]{:S(2)}) copy-start(f32[8,128,8]{1,2,0:T(8,128)} %copy-done.13) | copy-start | bytes 98308
  930.4 9.4 copy-start.1
  930.4 9.4 copy-start.8
  930.4 9.4 copy-start.9
  930.4 9.4 copy-start.17
Sparse Core Ops, SparseCore 0:
  26.8 329.0 all-gather.5
  470.3 326.4 all-gather.7
where the time goes:
time: 967 us; the launch traced here: 960 us
  waiting for transfers between devices  451 us (47%)
  other arithmetic  193 us (20%)
  matrix products  127 us (13%)
  local copies, waits for them, and re-layouts  117 us (12%)
  starting transfers between devices  34.8 us (4%)
  blocking collectives  22.2 us (2%)
  between operations  15 us (2%)
    all_gather x2, waiting for transfers between devices, prefix_2(): pieces = jax.tree.map(lambda part: lax.all_gather(part, axis), value)  369 us
    select_n x45, other arithmetic, lap(): jnp.where(position < mine, new, old)  179 us
    rev x2, local copies, waits for them, and re-layouts, prefix_2(): pieces = jax.tree.map(lambda part: part[::-1], pieces)  43.9 us
    unnamed x49, local copies, waits for them, and re-layouts  27.2 us
    all_gather x1, blocking collectives, prefix_2(): pieces = jax.tree.map(lambda part: lax.all_gather(part, axis), value)  22.2 us
    all_to_all x1, waiting for transfers between devices, per_device(): lax.all_to_all(query_cross, 'track', split_axis=1, concat_axis=0, tiled=T...  21.7 us
    all_to_all x1, waiting for transfers between devices, per_device(): lax.all_to_all(key_cross, 'track', split_axis=1, concat_axis=0, tiled=True)  20.3 us
  transfers between devices with their start and end apart: 9, of which 7 were waited for; matrix products, arithmetic and copies ran while one was open for 15% of the time, Pallas kernels for 0%

commit v1 on v0

v1 whole, which is shorter than its diff:
```python
import functools

import jax
import jax.numpy as jnp
from jax import lax
from jax.experimental import pallas as pl
from jax.experimental.pallas import tpu as pltpu
from jax.sharding import PartitionSpec as P


EPSILON = 1e-06
MESH = pl.DeviceIdType.MESH
BF = jnp.bfloat16
F32 = jnp.float32
HEADS_PER_CHUNK = 2


def mm(a, b):
    return lax.dot_general(a, b, (((1,), (0,)), ((), ())), preferred_element_type=F32)


def mm_nt(a, b):
    return lax.dot_general(a, b, (((1,), (1,)), ((), ())), preferred_element_type=F32)


def mm_tn(a, b):
    return lax.dot_general(a, b, (((0,), (0,)), ((), ())), preferred_element_type=F32)


def entry_barrier(me, count):
    barrier = pltpu.get_barrier_semaphore()

    @pl.when(me > 0)
    def _():
        pl.semaphore_signal(barrier, inc=1, device_id={"tm": me - 1}, device_id_type=MESH)

    @pl.when(me < count - 1)
    def _():
        pl.semaphore_signal(barrier, inc=1, device_id={"tm": me + 1}, device_id_type=MESH)

    peers = jnp.where(me > 0, 1, 0) + jnp.where(me < count - 1, 1, 0)
    pl.semaphore_wait(barrier, peers)


def chunk_copy(send_buf, recv_buf, send_sem, recv_sem, chunk, per, target):
    return pltpu.make_async_remote_copy(
        src_ref=send_buf.at[pl.ds(chunk * per, per)],
        dst_ref=recv_buf.at[pl.ds(chunk * per, per)],
        send_sem=send_sem.at[chunk],
        recv_sem=recv_sem.at[chunk],
        device_id={"tm": target},
        device_id_type=MESH,
    )


def forward_kernel(
    count, heads, per, q_ref, k_ref, v_ref, col_ref, row_ref, init_ref,
    normed_ref, out_ref, state_ref, recv_buf, send_buf, send_sem, recv_sem,
):
    me = lax.axis_index("tm")
    tracks, rows, width = q_ref.shape
    size = width // heads
    chunks = heads // per
    total = tracks * chunks
    target = jnp.minimum(me + 1, count - 1)
    entry_barrier(me, count)

    @pl.when(me == 0)
    def _():
        def fill(i, carry):
            recv_buf[pl.ds(i * heads, heads)] = init_ref[pl.ds(i * heads, heads)].astype(F32)
            return carry

        lax.fori_loop(0, tracks, fill, 0)

    t_index = lax.broadcasted_iota(jnp.int32, (rows, rows), 0)
    s_index = lax.broadcasted_iota(jnp.int32, (rows, rows), 1)
    lower = t_index >= s_index

    def one_track(x, carry):
        cols = col_ref[x]
        valid = cols[:, heads : heads + 1]
        from_start = jnp.exp(cols)
        to_end = jnp.exp(cols[rows - 1 : rows, :] - cols)
        for part in range(chunks):
            chunk = x * chunks + part
            sums = []
            keys = []
            for lane in range(per):
                h = part * per + lane
                cut = slice(h * size, (h + 1) * size)
                k_float = k_ref[x, :, cut].astype(F32) * valid
                keys.append(k_float.astype(BF))
                sums.append(mm_tn((k_float * to_end[:, h : h + 1]).astype(BF), v_ref[x, :, cut]))

            @pl.when(me > 0)
            def _():
                chunk_copy(send_buf, recv_buf, send_sem, recv_sem, chunk, per, target).wait_recv()

            for lane in range(per):
                h = part * per + lane
                slot = x * heads + h
                send_buf[slot] = (
                    from_start[rows - 1 : rows, h : h + 1] * recv_buf[slot] + sums[lane]
                )

            @pl.when(me < count - 1)
            def _():
                chunk_copy(send_buf, recv_buf, send_sem, recv_sem, chunk, per, target).start()

            for lane in range(per):
                h = part * per + lane
                slot = x * heads + h
                cut = slice(h * size, (h + 1) * size)
                q = q_ref[x, :, cut]
                state = recv_buf[slot].astype(BF)
                state_ref[slot] = state
                decay = jnp.exp(
                    jnp.where(lower, cols[:, h : h + 1] - row_ref[x, h : h + 1, :], -1e30)
                )
                scores = (mm_nt(q, keys[lane]) * decay).astype(BF)
                outputs = mm(scores, v_ref[x, :, cut]) + from_start[:, h : h + 1] * mm(q, state)
                square = jnp.mean(outputs * outputs, axis=-1, keepdims=True)
                inverse = lax.rsqrt(square + EPSILON) * valid
                normed_ref[x, :, cut] = (outputs * inverse).astype(BF)
                out_ref[x, :, cut] = outputs.astype(BF)
        return carry

    lax.fori_loop(0, tracks, one_track, 0)

    @pl.when(me < count - 1)
    def _():
        def drain(chunk, carry):
            chunk_copy(send_buf, recv_buf, send_sem, recv_sem, chunk, per, target).wait_send()
            return carry

        lax.fori_loop(0, total, drain, 0)


def backward_kernel(
    count, heads, per, q_ref, k_ref, v_ref, col_ref, row_ref, out_ref, gn_ref, state_ref,
    gq_ref, gk_ref, gv_ref, recv_buf, send_buf, send_sem, recv_sem,
):
    me = lax.axis_index("tm")
    tracks, rows, width = q_ref.shape
    size = width // heads
    chunks = heads // per
    total = tracks * chunks
    target = jnp.maximum(me - 1, 0)
    entry_barrier(me, count)

    @pl.when(me == count - 1)
    def _():
        def fill(i, carry):
            recv_buf[pl.ds(i * heads, heads)] = jnp.zeros((heads, size, size), F32)
            return carry

        lax.fori_loop(0, tracks, fill, 0)

    s_index = lax.broadcasted_iota(jnp.int32, (rows, rows), 0)
    t_index = lax.broadcasted_iota(jnp.int32, (rows, rows), 1)
    upper = t_index >= s_index

    def one_track(x, carry):
        cols = col_ref[x]
        valid = cols[:, heads : heads + 1]
        from_start = jnp.exp(cols)
        to_end = jnp.exp(cols[rows - 1 : rows, :] - cols)
        for part in range(chunks):
            chunk = x * chunks + part
            sums = []
            grads = []
            for lane in range(per):
                h = part * per + lane
                cut = slice(h * size, (h + 1) * size)
                outputs = out_ref[x, :, cut].astype(F32)
                square = jnp.mean(outputs * outputs, axis=-1, keepdims=True)
                inverse = lax.rsqrt(square + EPSILON)
                unit = outputs * inverse
                grad = gn_ref[x, :, cut].astype(F32)
                along = jnp.mean(grad * unit, axis=-1, keepdims=True)
                grad = ((inverse * valid) * (grad - unit * along)).astype(BF)
                grads.append(grad)
                q_from = (q_ref[x, :, cut].astype(F32) * from_start[:, h : h + 1]).astype(BF)
                sums.append(mm_tn(q_from, grad))

            @pl.when(me < count - 1)
            def _():
                chunk_copy(send_buf, recv_buf, send_sem, recv_sem, chunk, per, target).wait_recv()

            for lane in range(per):
                h = part * per + lane
                slot = x * heads + h
                send_buf[slot] = (
                    from_start[rows - 1 : rows, h : h + 1] * recv_buf[slot] + sums[lane]
                )

            @pl.when(me > 0)
            def _():
                chunk_copy(send_buf, recv_buf, send_sem, recv_sem, chunk, per, target).start()

            for lane in range(per):
                h = part * per + lane
                slot = x * heads + h
                cut = slice(h * size, (h + 1) * size)
                q = q_ref[x, :, cut]
                v = v_ref[x, :, cut]
                key = (k_ref[x, :, cut].astype(F32) * valid).astype(BF)
                grad = grads[lane]
                end_grad = recv_buf[slot].astype(BF)
                decay = jnp.exp(
                    jnp.where(upper, row_ref[x, h : h + 1, :] - cols[:, h : h + 1], -1e30)
                )
                grad_scores = (mm_nt(v, grad) * decay).astype(BF)
                scores = (mm_nt(key, q) * decay).astype(BF)
                grad_query = mm_tn(grad_scores, key)
                grad_query = grad_query + from_start[:, h : h + 1] * mm_nt(grad, state_ref[slot])
                gq_ref[x, :, cut] = grad_query.astype(BF)
                late = to_end[:, h : h + 1]
                grad_key = mm(grad_scores, q) + late * mm_nt(v, end_grad)
                gk_ref[x, :, cut] = (grad_key * valid).astype(BF)
                grad_value = mm(scores, grad) + late * mm(key, end_grad)
                gv_ref[x, :, cut] = grad_value.astype(BF)
        return carry

    lax.fori_loop(0, tracks, one_track, 0)

    @pl.when(me > 0)
    def _():
        def drain(chunk, carry):
            chunk_copy(send_buf, recv_buf, send_sem, recv_sem, chunk, per, target).wait_send()
            return carry

        lax.fori_loop(0, total, drain, 0)


def cross_kernel(groups, heads, scale, own_ref, bias_ref, *refs):
    q_refs, k_refs, g_refs, n_refs = (refs[i * groups : (i + 1) * groups] for i in range(4))
    outs = refs[4 * groups :]
    gn_outs, gq_outs, gk_outs = (outs[i * groups : (i + 1) * groups] for i in range(3))
    tracks, rows, width = q_refs[0].shape
    size = width // heads
    piece = tracks * rows

    def load(parts, cut):
        return jnp.concatenate([part[:, :, cut].reshape(piece, size) for part in parts], axis=0)

    def store(parts, cut, value):
        for i, part in enumerate(parts):
            part[:, :, cut] = value[i * piece : (i + 1) * piece].astype(BF).reshape(
                tracks, rows, size
            )

    bias = bias_ref[0]
    for h in range(heads):
        cut = slice(h * size, (h + 1) * size)
        q, k, g, n = (load(parts, cut) for parts in (q_refs, k_refs, g_refs, n_refs))
        logits = mm_nt(k, q) * scale + bias
        top = jnp.max(logits, axis=0, keepdims=True)
        weights = jnp.exp(logits - top)
        weights = weights * (1.0 / jnp.sum(weights, axis=0, keepdims=True))
        grad_weights = mm_nt(n, g)
        weighted = weights * grad_weights
        grad_logits = (weighted - weights * jnp.sum(weighted, axis=0, keepdims=True)) * scale
        grad_logits = grad_logits.astype(BF)
        store(gn_outs, cut, mm(weights.astype(BF), g))
        store(gq_outs, cut, mm_tn(grad_logits, k))
        store(gk_outs, cut, mm(grad_logits, q))


def per_device(
    count,
    groups,
    track_query,
    track_key,
    track_value,
    log_decay,
    valid_length,
    initial_state,
    cross_query,
    cross_key,
    grad_out,
):
    tracks, rows, width = track_query.shape
    heads = log_decay.shape[1]
    size = width // heads
    per = HEADS_PER_CHUNK if heads % HEADS_PER_CHUNK == 0 else 1
    chunks = heads // per
    slots = tracks * heads
    all_tracks = valid_length.shape[0]
    mine = lax.axis_index("track")
    time_first = lax.axis_index("tm") * rows
    piece_rows = rows // groups

    grouped = valid_length.reshape(groups, tracks)
    length_of = lambda group: lax.dynamic_index_in_dim(grouped, group, 0, keepdims=False)
    own_length = length_of(mine)
    times = time_first + jnp.arange(rows)
    valid = (times[None, :] < own_length[:, None]).astype(F32)

    triangle = (jnp.arange(rows)[:, None] <= jnp.arange(rows)[None, :]).astype(F32)
    within = jnp.einsum("xhs,st->xht", log_decay, triangle, precision=lax.Precision.HIGHEST)
    cols = jnp.concatenate(
        [
            jnp.transpose(within, (0, 2, 1)),
            valid[:, :, None],
            jnp.zeros((tracks, rows, 128 - heads - 1), F32),
        ],
        axis=2,
    )

    def piece_of(value, group):
        return lax.dynamic_slice_in_dim(value, group * piece_rows, piece_rows, axis=1)

    def send(value, shift):
        perm = [(i, (i + shift) % groups) for i in range(groups)]
        return lax.ppermute(piece_of(value, (mine + shift) % groups), "track", perm)

    grad_masked = grad_out * valid[:, :, None].astype(BF)
    q_parts = [cross_query] + [send(cross_query, s) for s in range(1, groups)]
    k_parts = [cross_key] + [send(cross_key, s) for s in range(1, groups)]
    g_parts = [grad_masked] + [send(grad_masked, s) for s in range(1, groups)]

    vmem = pl.BlockSpec(memory_space=pltpu.VMEM)
    wide = jax.ShapeDtypeStruct((tracks, rows, width), BF)
    scratch = [
        pltpu.VMEM((slots, size, size), F32),
        pltpu.VMEM((slots, size, size), F32),
        pltpu.SemaphoreType.DMA((tracks * chunks,)),
        pltpu.SemaphoreType.DMA((tracks * chunks,)),
    ]
    dot_flops = 2 * slots * rows * size * size
    normed, outputs, states = pl.pallas_call(
        functools.partial(forward_kernel, count, heads, per),
        out_shape=(wide, wide, jax.ShapeDtypeStruct((slots, size, size), BF)),
        in_specs=[vmem] * 6,
        out_specs=(vmem,) * 3,
        scratch_shapes=scratch,
        compiler_params=pltpu.CompilerParams(
            collective_id=0, has_side_effects=True, vmem_limit_bytes=56 * 2**20
        ),
        cost_estimate=pl.CostEstimate(
            flops=400 * dot_flops, bytes_accessed=16 * slots * size * size, transcendentals=0
        ),
        name="forward_chain",
    )(track_query, track_key, track_value, cols, within, initial_state.reshape(slots, size, size))

    n_parts = [normed] + [send(normed, s) for s in range(1, groups)]

    tile = min(16, piece_rows)
    tiles = piece_rows // tile
    lengths = jnp.concatenate([length_of((mine - s) % groups) for s in range(groups)])
    tile_times = (
        time_first + mine * piece_rows + jnp.arange(piece_rows).reshape(tiles, 1, tile)
    )
    key_valid = (tile_times < lengths[None, :, None]).reshape(tiles, all_tracks * tile, 1)
    row_time = jnp.arange(all_tracks * tile) % tile
    same_time = row_time[:, None] == row_time[None, :]
    bias = jnp.where(key_valid & same_time[None], 0.0, -1e30).astype(F32)
    own_block = jnp.reshape(mine * tiles, (1,)).astype(jnp.int32)

    own_spec = pl.BlockSpec((tracks, tile, width), lambda t, own: (0, own[0] + t, 0))
    other_spec = pl.BlockSpec((tracks, tile, width), lambda t, own: (0, t, 0))
    bias_spec = pl.BlockSpec(
        (1, all_tracks * tile, all_tracks * tile), lambda t, own: (t, 0, 0)
    )
    piece_shape = jax.ShapeDtypeStruct((tracks, piece_rows, width), BF)
    cross = pl.pallas_call(
        functools.partial(cross_kernel, groups, heads, 1.0 / float(size) ** 0.5),
        out_shape=(piece_shape,) * (3 * groups),
        grid_spec=pltpu.PrefetchScalarGridSpec(
            num_scalar_prefetch=1,
            grid=(tiles,),
            in_specs=[bias_spec] + ([own_spec] + [other_spec] * (groups - 1)) * 4,
            out_specs=(other_spec,) * (3 * groups),
        ),
        compiler_params=pltpu.CompilerParams(vmem_limit_bytes=56 * 2**20),
        cost_estimate=pl.CostEstimate(
            flops=100 * dot_flops, bytes_accessed=16 * slots * size * size, transcendentals=0
        ),
        name="cross_attention",
    )(own_block, bias, *q_parts, *k_parts, *g_parts, *n_parts)

    def collect(parts):
        whole = jnp.zeros((tracks, rows, width), BF)
        for s, part in enumerate(parts):
            if s:
                perm = [(i, (i - s) % groups) for i in range(groups)]
                part = lax.ppermute(part, "track", perm)
            start = ((mine + s) % groups) * piece_rows
            whole = lax.dynamic_update_slice_in_dim(whole, part, start, axis=1)
        return whole

    grad_normed = collect(cross[:groups])
    grad_cross_query = collect(cross[groups : 2 * groups])
    grad_cross_key = collect(cross[2 * groups :])

    grad_query, grad_key, grad_value = pl.pallas_call(
        functools.partial(backward_kernel, count, heads, per),
        out_shape=(wide,) * 3,
        in_specs=[vmem] * 8,
        out_specs=(vmem,) * 3,
        scratch_shapes=scratch,
        compiler_params=pltpu.CompilerParams(
            collective_id=1, has_side_effects=True, vmem_limit_bytes=60 * 2**20
        ),
        cost_estimate=pl.CostEstimate(
            flops=400 * dot_flops, bytes_accessed=16 * slots * size * size, transcendentals=0
        ),
        name="backward_chain",
    )(track_query, track_key, track_value, cols, within, outputs, grad_normed, states)
    return grad_query, grad_key, grad_value, grad_cross_query, grad_cross_key


def solution(mesh):
    wide = P("track", "tm", None)
    return jax.shard_map(
        functools.partial(per_device, mesh.shape["tm"], mesh.shape["track"]),
        mesh=mesh,
        in_specs=(
            wide,
            wide,
            wide,
            P("track", None, "tm"),
            P(),
            P("track", None, None, None),
            wide,
            wide,
            wide,
        ),
        out_specs=(wide,) * 5,
        check_vma=False,
    )
```

time: 967 us -> 334 us (0.35)
  waiting for transfers between devices: 451 us -> 69 us
  Pallas kernels: 0 us -> 230 us
  other arithmetic: 193 us -> 2.77 us
  matrix products: 127 us -> 0.17 us
  local copies, waits for them, and re-layouts: 117 us -> 21.9 us
  starting transfers between devices: 34.8 us -> 9.24 us
  blocking collectives: 22.2 us -> 0 us
  between operations: 15 us -> 1.01 us
    all_gather x2 -> x0, waiting for transfers between devices: 369 us -> none  [prefix_2(): pieces = jax.tree.map(lambda part: lax.all_gather(part, axis), value)]
    pallas_call x0 -> x3, Pallas kernels: none -> 230 us  [the longest x1 183 us: per_device(): pl.pallas_call(functools.partial(backward_kernel, count, heads, per), out...]
    select_n x45 -> x2, other arithmetic: 179 us -> 1.18 us  [the longest x1 1.18 us: per_device(): bias = jnp.where(key_valid & same_time[None], 0.0, -1e+30).astype(F32)]
    dot_general x17 -> x1, matrix products: 127 us -> 0.17 us  [per_device(): jnp.einsum('xhs,st->xht', log_decay, triangle, precision=lax.Precision.HI...]
    all_to_all x7 -> x0, waiting for transfers between devices: 81.4 us -> none  [the longest x1 21.7 us: per_device(): lax.all_to_all(query_cross, 'track', split_axis=1, concat_axis=0, tiled=T...]
    ppermute x0 -> x7, waiting for transfers between devices: none -> 69 us  [the longest x4 58.6 us: send(): return lax.ppermute(piece_of(value, (mine + shift) % groups), 'track', perm)]
    rev x2 -> x0, local copies, waits for them, and re-layouts: 43.9 us -> none  [prefix_2(): pieces = jax.tree.map(lambda part: part[::-1], pieces)]
    all_to_all x7 -> x0, starting transfers between devices: 34.7 us -> none  [the longest x1 5.19 us: per_device(): lax.all_to_all(normed, 'track', split_axis=1, concat_axis=0, tiled=True)]
  transfers between devices with their start and end apart: 9 -> 7, of which waited for: 7 -> 5; matrix products, arithmetic and copies ran while one was open for 15% -> 2% of each run, Pallas kernels for 0% -> 55%
where the time goes in v1:
time: 334 us
  Pallas kernels  230 us (69%)
  waiting for transfers between devices  69 us (21%)
  local copies, waits for them, and re-layouts  21.9 us (7%)
  starting transfers between devices  9.24 us (3%)
    pallas_call x1, Pallas kernels, per_device(): pl.pallas_call(functools.partial(backward_kernel, count, heads, per), out...  183 us
    ppermute x4, waiting for transfers between devices, send(): return lax.ppermute(piece_of(value, (mine + shift) % groups), 'track', perm)  58.6 us
    pallas_call x1, Pallas kernels, per_device(): pl.pallas_call(functools.partial(forward_kernel, count, heads, per), out_...  29 us
    pallas_call x1, Pallas kernels, per_device(): pl.pallas_call(functools.partial(cross_kernel, groups, heads, 1.0 / float...  18 us
    unnamed x37, local copies, waits for them, and re-layouts  13 us
    ppermute x3, waiting for transfers between devices, collect(): part = lax.ppermute(part, 'track', perm)  10.4 us
  transfers between devices with their start and end apart: 7, of which 5 were waited for; matrix products, arithmetic and copies ran while one was open for 2% of the time, Pallas kernels for 55%

profile of v1, /device:TPU:0, one launch (start us, length us, event | category | flops | bytes accessed | tf_op | source)
XLA Modules:
  0.0 334.0 jit_solution(11282531946451582811)
XLA Ops:
  0.7 0.7 reshape.188
  2.0 1.0 maximum_maximum_fusion.col_ref
  3.1 29.0 %forward_chain.1 = (bf16[8,128,1024]{2,1,0:T(8,128)(2,1)}, bf16[8,128,1024]{2,1,0:T(8,128)(2,1)}, bf16[64,128,128]{2,1,0:T(8,128)(2,1)}) custom-call(bf16[8,128,1024]{2,1,0:T(8,128)(2,1)} %q_ref.3, bf16[8,128,1024]{2,1,0:T(8,128)(2,1)} %k_ref.3, bf16[8,128,1024]{2,1,0:T(8,128)(2,1)} %v_ref.3, f32[8,128,128]{2,1,0:T(8,128)} %maximum_maximum_fusion.col_ref, ...), custom_call_target="tpu_custom_call" | custom-call | flops 107374182400 | bytes 16777216 | tf_op jit(solution)/shard_map/forward_chain/pallas_call | solution.py:333
  32.1 1.5 constant_dynamic-slice_fusion
  33.6 2.6 collective-permute-start.3
  36.5 0.3 collective-permute-start.2
  36.9 1.9 copy-done.14
  38.9 0.3 collective-permute-start
  39.4 1.1 constant_dynamic-slice_fusion.2
  40.5 1.5 collective-permute-start.1
  42.5 1.2 and_select_fusion.bias_ref
  43.7 5.3 %collective-permute-done.3.refs_7_ = bf16[8,64,1024]{2,1,0:T(8,128)(2,1)} collective-permute-done((bf16[8,64,1024]{2,1,0:T(8,128)(2,1)S(1)}, bf16[8,64,1024]{2,1,0:T(8,128)(2,1)}, u32[]{:S(2)}, u32[]{:S(2)}) %collective-permute-start.3) | collective-permute-done | bytes 1048608 | tf_op jit(solution)/shard_map/ppermute | solution.py:317
  49.0 11.2 %collective-permute-done.2.refs_5_ = bf16[8,64,1024]{2,1,0:T(8,128)(2,1)} collective-permute-done((bf16[8,64,1024]{2,1,0:T(8,128)(2,1)S(1)}, bf16[8,64,1024]{2,1,0:T(8,128)(2,1)}, u32[]{:S(2)}, u32[]{:S(2)}) %collective-permute-start.2) | collective-permute-done | bytes 1048608 | tf_op jit(solution)/shard_map/ppermute | solution.py:317
  60.2 19.6 %collective-permute-done.refs_1_ = bf16[8,64,1024]{2,1,0:T(8,128)(2,1)} collective-permute-done((bf16[8,64,1024]{2,1,0:T(8,128)(2,1)S(1)}, bf16[8,64,1024]{2,1,0:T(8,128)(2,1)}, u32[]{:S(2)}, u32[]{:S(2)}) %collective-permute-start) | collective-permute-done | bytes 1048608 | tf_op jit(solution)/shard_map/ppermute | solution.py:317
  79.8 22.5 %collective-permute-done.1.refs_3_ = bf16[8,64,1024]{2,1,0:T(8,128)(2,1)} collective-permute-done((bf16[8,64,1024]{2,1,0:T(8,128)(2,1)}, bf16[8,64,1024]{2,1,0:T(8,128)(2,1)}, u32[]{:S(2)}, u32[]{:S(2)}) %collective-permute-start.1) | collective-permute-done | bytes 1048608 | tf_op jit(solution)/shard_map/ppermute | solution.py:317
  102.3 18.0 %cross_attention.1 = (bf16[8,64,1024]{2,1,0:T(8,128)(2,1)}, bf16[8,64,1024]{2,1,0:T(8,128)(2,1)}, bf16[8,64,1024]{2,1,0:T(8,128)(2,1)}, bf16[8,64,1024]{2,1,0:T(...) custom-call(s32[1]{0:T(128)} %bitcast.5.own_ref, f32[4,256,256]{2,1,0:T(8,128)} %and_select_fusion.bias_ref, ...), custom_call_target="tpu_custom_call" | custom-call | flops 26843545600 | bytes 16777216 | tf_op jit(solution)/shard_map/cross_attention/pallas_call | solution.py:368
  120.3 2.4 collective-permute-start.4
  122.8 1.9 collective-permute-start.5
  125.2 0.3 broadcast.149.clone.1
  125.4 1.3 copy-done.12
  127.1 1.3 copy-done.11
  128.5 10.4 %collective-permute-done.4 = bf16[8,64,1024]{2,1,0:T(8,128)(2,1)} collective-permute-done((bf16[8,64,1024]{2,1,0:T(8,128)(2,1)}, bf16[8,64,1024]{2,1,0:T(8,128)(2,1)}, u32[]{:S(2)}, u32[]{:S(2)}) %collective-permute-start.4) | collective-permute-done | bytes 1048608 | tf_op jit(solution)/shard_map/ppermute | solution.py:389
  138.9 1.3 constant_dynamic-update-slice_fusion.4.gn_ref
  140.2 1.3 copy-done.2
  141.5 182.9 %backward_chain.1 = (bf16[8,128,1024]{2,1,0:T(8,128)(2,1)}, bf16[8,128,1024]{2,1,0:T(8,128)(2,1)}, bf16[8,128,1024]{2,1,0:T(8,128)(2,1)}) custom-call(bf16[8,128,1024]{2,1,0:T(8,128)(2,1)} %q_ref.3, bf16[8,128,1024]{2,1,0:T(8,128)(2,1)} %k_ref.3, bf16[8,128,1024]{2,1,0:T(8,128)(2,1)} %v_ref.3, f32[8,128,128]{2,1,0:T(8,128)} %maximum_maximum_fusion.col_ref, ...), custom_call_target="tpu_custom_call" | custom-call | flops 107374182400 | bytes 16777216 | tf_op jit(solution)/shard_map/backward_chain/pallas_call | solution.py:398
  324.5 2.4 constant_dynamic-update-slice_fusion
  327.2 1.3 copy.26
  328.5 0.8 copy-done.6
  329.3 1.0 copy-done.8
  330.3 1.3 copy.27
  331.6 1.0 copy-done.7
  332.6 1.3 copy.28
  (56 shorter events, 2.9 us)
Async XLA Ops:
  0.6 0.8 copy-start
  1.6 1.5 copy-start.16
  32.0 4.1 %copy-start.10 = (bf16[8,128,1024]{2,1,0:T(8,128)(2,1)S(1)}, bf16[8,128,1024]{2,1,0:T(8,128)(2,1)}, u32[]{:S(2)}) copy-start(bf16[8,128,1024]{2,1,0:T(8,128)(2,1)} %param.17) | copy-start | bytes 6291460
  33.6 15.5 %collective-permute-start.3 = (bf16[8,64,1024]{2,1,0:T(8,128)(2,1)S(1)}, bf16[8,64,1024]{2,1,0:T(8,128)(2,1)}, u32[]{:S(2)}, u32[]{:S(2)}) collective-permute-start(bf16[8,64,1024]{2,1,0:T(8,128)(2,1)S(1)} %constant_dynamic-slice_fusion), channel_id=1, source_target_pairs={{0,16},{16,0},{1,17},{17,1},{2,18},{18,2},{3,19},{19,3},{4,20},{20... | collective-permute-start | bytes 3145736 | tf_op jit(solution)/shard_map/ppermute | solution.py:317
  36.4 2.4 copy-start.1
  36.4 2.4 copy-start.14
  36.4 3.0 copy-start.15
  36.5 23.7 %collective-permute-start.2 = (bf16[8,64,1024]{2,1,0:T(8,128)(2,1)S(1)}, bf16[8,64,1024]{2,1,0:T(8,128)(2,1)}, u32[]{:S(2)}, u32[]{:S(2)}) collective-permute-start(bf16[8,64,1024]{2,1,0:T(8,128)(2,1)S(1)} %constant_dynamic-slice_fusion.1), channel_id=1, source_target_pairs={{0,16},{16,0},{1,17},{17,1},{2,18},{18,2},{3,19},{19,3},{4,20},{20... | collective-permute-start | bytes 3145736 | tf_op jit(solution)/shard_map/ppermute | solution.py:317
  38.9 40.9 %collective-permute-start = (bf16[8,64,1024]{2,1,0:T(8,128)(2,1)S(1)}, bf16[8,64,1024]{2,1,0:T(8,128)(2,1)}, u32[]{:S(2)}, u32[]{:S(2)}) collective-permute-start(bf16[8,64,1024]{2,1,0:T(8,128)(2,1)S(1)} %constant_dynamic-slice_fusion.3), channel_id=1, source_target_pairs={{0,16},{16,0},{1,17},{17,1},{2,18},{18,2},{3,19},{19,3},{4,20},{20... | collective-permute-start | bytes 3145736 | tf_op jit(solution)/shard_map/ppermute | solution.py:317
  40.5 61.8 %collective-permute-start.1 = (bf16[8,64,1024]{2,1,0:T(8,128)(2,1)}, bf16[8,64,1024]{2,1,0:T(8,128)(2,1)}, u32[]{:S(2)}, u32[]{:S(2)}) collective-permute-start(bf16[8,64,1024]{2,1,0:T(8,128)(2,1)} %constant_dynamic-slice_fusion.2), channel_id=1, source_target_pairs={{0,16},{16,0},{1,17},{17,1},{2,18},{18,2},{3,19},{19,3},{4,20},{20... | collective-permute-start | bytes 3145736 | tf_op jit(solution)/shard_map/ppermute | solution.py:317
  120.3 4.7 %copy-start.13 = (bf16[8,64,1024]{2,1,0:T(8,128)(2,1)S(1)}, bf16[8,64,1024]{2,1,0:T(8,128)(2,1)}, u32[]{:S(2)}) copy-start(bf16[8,64,1024]{2,1,0:T(8,128)(2,1)} %get-tuple-element.27) | copy-start | bytes 3145732
  120.3 18.6 %collective-permute-start.4 = (bf16[8,64,1024]{2,1,0:T(8,128)(2,1)}, bf16[8,64,1024]{2,1,0:T(8,128)(2,1)}, u32[]{:S(2)}, u32[]{:S(2)}) collective-permute-start(bf16[8,64,1024]{2,1,0:T(8,128)(2,1)} %get-tuple-element.20), channel_id=1, source_target_pairs={{0,16},{16,0},{1,17},{17,1},{2,18},{18,2},{3,19},{19,3},{4,20},{20... | collective-permute-start | bytes 3145736 | tf_op jit(solution)/shard_map/ppermute | solution.py:389
  122.7 201.7 %collective-permute-start.6 = (bf16[8,64,1024]{2,1,0:T(8,128)(2,1)}, bf16[8,64,1024]{2,1,0:T(8,128)(2,1)}, u32[]{:S(2)}, u32[]{:S(2)}) collective-permute-start(bf16[8,64,1024]{2,1,0:T(8,128)(2,1)} %get-tuple-element.28), channel_id=1, source_target_pairs={{0,16},{16,0},{1,17},{17,1},{2,18},{18,2},{3,19},{19,3},{4,20},{20... | collective-permute-start | bytes 3145736 | tf_op jit(solution)/shard_map/ppermute | solution.py:389
  122.8 204.1 %collective-permute-start.5 = (bf16[8,64,1024]{2,1,0:T(8,128)(2,1)}, bf16[8,64,1024]{2,1,0:T(8,128)(2,1)S(1)}, u32[]{:S(2)}, u32[]{:S(2)}) collective-permute-start(bf16[8,64,1024]{2,1,0:T(8,128)(2,1)} %get-tuple-element.26), channel_id=1, source_target_pairs={{0,16},{16,0},{1,17},{17,1},{2,18},{18,2},{3,19},{19,3},{4,20},{20... | collective-permute-start | bytes 3145736 | tf_op jit(solution)/shard_map/ppermute | solution.py:389
  125.0 1.7 copy-start.12
  125.1 1.7 copy-start.3
  126.7 1.7 copy-start.11
  126.8 1.7 copy-start.4
  140.2 1.3 copy-start.2
  324.5 2.5 copy-start.5
  324.5 2.7 copy-start.9
  327.2 2.1 copy-start.6
  327.2 3.1 copy-start.8
  330.3 2.3 copy-start.7

commit v2 on v1

--- a/solution.py
+++ b/solution.py
@@ -12,7 +12,8 @@
 MESH = pl.DeviceIdType.MESH
 BF = jnp.bfloat16
 F32 = jnp.float32
-HEADS_PER_CHUNK = 2
+HEADS_PER_CHUNK = 1
+PARTS = 2
 
 
 def mm(a, b):
@@ -53,8 +54,13 @@
     )
 
 
+def split(value):
+    high = value.astype(BF)
+    return high, (value - high.astype(F32)).astype(BF)
+
+
 def forward_kernel(
-    count, heads, per, q_ref, k_ref, v_ref, col_ref, row_ref, init_ref,
+    count, heads, first, lanes, per, q_ref, k_ref, v_ref, col_ref, row_ref, init_ref,
     normed_ref, out_ref, state_ref, recv_buf, send_buf, send_sem, recv_sem,
 ):
     me = lax.axis_index("tm")
@@ -68,7 +74,7 @@
     @pl.when(me == 0)
     def _():
         def fill(i, carry):
-            recv_buf[pl.ds(i * heads, heads)] = init_ref[pl.ds(i * heads, heads)].astype(F32)
+            recv_buf[pl.ds(i * heads, heads)] = init_ref[i].astype(F32)
             return carry
 
         lax.fori_loop(0, tracks, fill, 0)
@@ -79,7 +85,7 @@
 
     def one_track(x, carry):
         cols = col_ref[x]
-        valid = cols[:, heads : heads + 1]
+        valid = cols[:, lanes : lanes + 1]
         from_start = jnp.exp(cols)
         to_end = jnp.exp(cols[rows - 1 : rows, :] - cols)
         for part in range(chunks):
@@ -91,7 +97,9 @@
                 cut = slice(h * size, (h + 1) * size)
                 k_float = k_ref[x, :, cut].astype(F32) * valid
                 keys.append(k_float.astype(BF))
-                sums.append(mm_tn((k_float * to_end[:, h : h + 1]).astype(BF), v_ref[x, :, cut]))
+                high, low = split(k_float * to_end[:, first + h : first + h + 1])
+                v = v_ref[x, :, cut]
+                sums.append(mm_tn(high, v) + mm_tn(low, v))
 
             @pl.when(me > 0)
             def _():
@@ -101,7 +109,7 @@
                 h = part * per + lane
                 slot = x * heads + h
                 send_buf[slot] = (
-                    from_start[rows - 1 : rows, h : h + 1] * recv_buf[slot] + sums[lane]
+                    from_start[rows - 1 : rows, first + h : first + h + 1] * recv_buf[slot] + sums[lane]
                 )
 
             @pl.when(me < count - 1)
@@ -113,13 +121,16 @@
                 slot = x * heads + h
                 cut = slice(h * size, (h + 1) * size)
                 q = q_ref[x, :, cut]
-                state = recv_buf[slot].astype(BF)
+                state, state_low = split(recv_buf[slot])
                 state_ref[slot] = state
                 decay = jnp.exp(
-                    jnp.where(lower, cols[:, h : h + 1] - row_ref[x, h : h + 1, :], -1e30)
+                    jnp.where(lower, cols[:, first + h : first + h + 1] - row_ref[x, first + h : first + h + 1, :], -1e30)
                 )
-                scores = (mm_nt(q, keys[lane]) * decay).astype(BF)
-                outputs = mm(scores, v_ref[x, :, cut]) + from_start[:, h : h + 1] * mm(q, state)
+                scores, scores_low = split(mm_nt(q, keys[lane]) * decay)
+                v = v_ref[x, :, cut]
+                late = mm(q, state) + mm(q, state_low)
+                outputs = mm(scores, v) + mm(scores_low, v)
+                outputs = outputs + from_start[:, first + h : first + h + 1] * late
                 square = jnp.mean(outputs * outputs, axis=-1, keepdims=True)
                 inverse = lax.rsqrt(square + EPSILON) * valid
                 normed_ref[x, :, cut] = (outputs * inverse).astype(BF)
@@ -138,7 +149,7 @@
 
 
 def backward_kernel(
-    count, heads, per, q_ref, k_ref, v_ref, col_ref, row_ref, out_ref, gn_ref, state_ref,
+    count, heads, first, lanes, per, q_ref, k_ref, v_ref, col_ref, row_ref, out_ref, gn_ref, state_ref,
     gq_ref, gk_ref, gv_ref, recv_buf, send_buf, send_sem, recv_sem,
 ):
     me = lax.axis_index("tm")
@@ -163,7 +174,7 @@
 
     def one_track(x, carry):
         cols = col_ref[x]
-        valid = cols[:, heads : heads + 1]
+        valid = cols[:, lanes : lanes + 1]
         from_start = jnp.exp(cols)
         to_end = jnp.exp(cols[rows - 1 : rows, :] - cols)
         for part in range(chunks):
@@ -181,7 +192,7 @@
                 along = jnp.mean(grad * unit, axis=-1, keepdims=True)
                 grad = ((inverse * valid) * (grad - unit * along)).astype(BF)
                 grads.append(grad)
-                q_from = (q_ref[x, :, cut].astype(F32) * from_start[:, h : h + 1]).astype(BF)
+                q_from = (q_ref[x, :, cut].astype(F32) * from_start[:, first + h : first + h + 1]).astype(BF)
                 sums.append(mm_tn(q_from, grad))
 
             @pl.when(me < count - 1)
@@ -192,7 +203,7 @@
                 h = part * per + lane
                 slot = x * heads + h
                 send_buf[slot] = (
-                    from_start[rows - 1 : rows, h : h + 1] * recv_buf[slot] + sums[lane]
+                    from_start[rows - 1 : rows, first + h : first + h + 1] * recv_buf[slot] + sums[lane]
                 )
 
             @pl.when(me > 0)
@@ -209,14 +220,14 @@
                 grad = grads[lane]
                 end_grad = recv_buf[slot].astype(BF)
                 decay = jnp.exp(
-                    jnp.where(upper, row_ref[x, h : h + 1, :] - cols[:, h : h + 1], -1e30)
+                    jnp.where(upper, row_ref[x, first + h : first + h + 1, :] - cols[:, first + h : first + h + 1], -1e30)
                 )
                 grad_scores = (mm_nt(v, grad) * decay).astype(BF)
                 scores = (mm_nt(key, q) * decay).astype(BF)
                 grad_query = mm_tn(grad_scores, key)
-                grad_query = grad_query + from_start[:, h : h + 1] * mm_nt(grad, state_ref[slot])
+                grad_query = grad_query + from_start[:, first + h : first + h + 1] * mm_nt(grad, state_ref[slot])
                 gq_ref[x, :, cut] = grad_query.astype(BF)
-                late = to_end[:, h : h + 1]
+                late = to_end[:, first + h : first + h + 1]
                 grad_key = mm(grad_scores, q) + late * mm_nt(v, end_grad)
                 gk_ref[x, :, cut] = (grad_key * valid).astype(BF)
                 grad_value = mm(scores, grad) + late * mm(key, end_grad)
@@ -284,9 +295,12 @@
     tracks, rows, width = track_query.shape
     heads = log_decay.shape[1]
     size = width // heads
-    per = HEADS_PER_CHUNK if heads % HEADS_PER_CHUNK == 0 else 1
-    chunks = heads // per
-    slots = tracks * heads
+    parts = PARTS if heads % PARTS == 0 else 1
+    part_heads = heads // parts
+    part_width = width // parts
+    per = HEADS_PER_CHUNK if part_heads % HEADS_PER_CHUNK == 0 else 1
+    chunks = part_heads // per
+    slots = tracks * part_heads
     all_tracks = valid_length.shape[0]
     mine = lax.axis_index("track")
     time_first = lax.axis_index("tm") * rows
@@ -309,20 +323,29 @@
         axis=2,
     )
 
-    def piece_of(value, group):
-        return lax.dynamic_slice_in_dim(value, group * piece_rows, piece_rows, axis=1)
-
     def send(value, shift):
         perm = [(i, (i + shift) % groups) for i in range(groups)]
-        return lax.ppermute(piece_of(value, (mine + shift) % groups), "track", perm)
+        start = ((mine + shift) % groups) * piece_rows
+        piece = lax.dynamic_slice_in_dim(value, start, piece_rows, axis=1)
+        return lax.ppermute(piece, "track", perm)
 
     grad_masked = grad_out * valid[:, :, None].astype(BF)
     q_parts = [cross_query] + [send(cross_query, s) for s in range(1, groups)]
     k_parts = [cross_key] + [send(cross_key, s) for s in range(1, groups)]
     g_parts = [grad_masked] + [send(grad_masked, s) for s in range(1, groups)]
 
-    vmem = pl.BlockSpec(memory_space=pltpu.VMEM)
-    wide = jax.ShapeDtypeStruct((tracks, rows, width), BF)
+    once = pl.Buffered(1)
+
+    def wide_spec(part):
+        return pl.BlockSpec(
+            (tracks, rows, part_width), lambda i: (0, 0, part), pipeline_mode=once
+        )
+
+    narrow_spec = wide_spec(0)
+    col_spec = pl.BlockSpec((tracks, rows, 128), lambda i: (0, 0, 0), pipeline_mode=once)
+    row_spec = pl.BlockSpec((tracks, heads, rows), lambda i: (0, 0, 0), pipeline_mode=once)
+    state_spec = pl.BlockSpec((slots, size, size), lambda i: (0, 0, 0), pipeline_mode=once)
+    narrow = jax.ShapeDtypeStruct((tracks, rows, part_width), BF)
     scratch = [
         pltpu.VMEM((slots, size, size), F32),
         pltpu.VMEM((slots, size, size), F32),
@@ -330,22 +353,37 @@
         pltpu.SemaphoreType.DMA((tracks * chunks,)),
     ]
     dot_flops = 2 * slots * rows * size * size
-    normed, outputs, states = pl.pallas_call(
-        functools.partial(forward_kernel, count, heads, per),
-        out_shape=(wide, wide, jax.ShapeDtypeStruct((slots, size, size), BF)),
-        in_specs=[vmem] * 6,
-        out_specs=(vmem,) * 3,
-        scratch_shapes=scratch,
-        compiler_params=pltpu.CompilerParams(
-            collective_id=0, has_side_effects=True, vmem_limit_bytes=56 * 2**20
-        ),
-        cost_estimate=pl.CostEstimate(
-            flops=400 * dot_flops, bytes_accessed=16 * slots * size * size, transcendentals=0
-        ),
-        name="forward_chain",
-    )(track_query, track_key, track_value, cols, within, initial_state.reshape(slots, size, size))
-
-    n_parts = [normed] + [send(normed, s) for s in range(1, groups)]
+
+    def estimate(times_over):
+        return pl.CostEstimate(
+            flops=times_over * dot_flops,
+            bytes_accessed=16 * slots * size * size,
+            transcendentals=0,
+        )
+
+    forward = []
+    for part in range(parts):
+        init_spec = pl.BlockSpec(
+            (tracks, part_heads, size, size),
+            functools.partial(lambda part, i: (0, part, 0, 0), part),
+            pipeline_mode=once,
+        )
+        forward.append(
+            pl.pallas_call(
+                functools.partial(forward_kernel, count, part_heads, part * part_heads, heads, per),
+                out_shape=(narrow, narrow, jax.ShapeDtypeStruct((slots, size, size), BF)),
+                grid=(1,),
+                in_specs=[wide_spec(part)] * 3 + [col_spec, row_spec, init_spec],
+                out_specs=(narrow_spec, narrow_spec, state_spec),
+                scratch_shapes=scratch,
+                compiler_params=pltpu.CompilerParams(
+                    collective_id=part,
+                    has_side_effects=True,
+                    vmem_limit_bytes=48 * 2**20,
+                ),
+                cost_estimate=estimate(400),
+            )(track_query, track_key, track_value, cols, within, initial_state)
+        )
 
     tile = min(16, piece_rows)
     tiles = piece_rows // tile
@@ -358,58 +396,100 @@
     same_time = row_time[:, None] == row_time[None, :]
     bias = jnp.where(key_valid & same_time[None], 0.0, -1e30).astype(F32)
     own_block = jnp.reshape(mine * tiles, (1,)).astype(jnp.int32)
-
-    own_spec = pl.BlockSpec((tracks, tile, width), lambda t, own: (0, own[0] + t, 0))
-    other_spec = pl.BlockSpec((tracks, tile, width), lambda t, own: (0, t, 0))
     bias_spec = pl.BlockSpec(
         (1, all_tracks * tile, all_tracks * tile), lambda t, own: (t, 0, 0)
     )
-    piece_shape = jax.ShapeDtypeStruct((tracks, piece_rows, width), BF)
-    cross = pl.pallas_call(
-        functools.partial(cross_kernel, groups, heads, 1.0 / float(size) ** 0.5),
-        out_shape=(piece_shape,) * (3 * groups),
-        grid_spec=pltpu.PrefetchScalarGridSpec(
-            num_scalar_prefetch=1,
-            grid=(tiles,),
-            in_specs=[bias_spec] + ([own_spec] + [other_spec] * (groups - 1)) * 4,
-            out_specs=(other_spec,) * (3 * groups),
-        ),
-        compiler_params=pltpu.CompilerParams(vmem_limit_bytes=56 * 2**20),
-        cost_estimate=pl.CostEstimate(
-            flops=100 * dot_flops, bytes_accessed=16 * slots * size * size, transcendentals=0
-        ),
-        name="cross_attention",
-    )(own_block, bias, *q_parts, *k_parts, *g_parts, *n_parts)
-
-    def collect(parts):
-        whole = jnp.zeros((tracks, rows, width), BF)
-        for s, part in enumerate(parts):
-            if s:
-                perm = [(i, (i - s) % groups) for i in range(groups)]
-                part = lax.ppermute(part, "track", perm)
-            start = ((mine + s) % groups) * piece_rows
-            whole = lax.dynamic_update_slice_in_dim(whole, part, start, axis=1)
+    result_spec = pl.BlockSpec((tracks, tile, part_width), lambda t, own: (0, t, 0))
+    piece_shape = jax.ShapeDtypeStruct((tracks, piece_rows, part_width), BF)
+
+    back_perms = [[(i, (i - s) % groups) for i in range(groups)] for s in range(groups)]
+
+    def returned(pieces):
+        return [
+            lax.ppermute(piece, "track", back_perms[s]) if s else piece
+            for s, piece in enumerate(pieces)
+        ]
+
+    n_all = []
+    for part in range(parts):
+        normed = forward[part][0]
+        n_all.append([normed] + [send(normed, s) for s in range(1, groups)])
+
+    gn_all, gq_all, gk_all = [], [], []
+    for part in range(parts):
+        own_spec = pl.BlockSpec(
+            (tracks, tile, part_width),
+            functools.partial(lambda part, t, own: (0, own[0] + t, part), part),
+        )
+        other_spec = pl.BlockSpec(
+            (tracks, tile, part_width), functools.partial(lambda part, t, own: (0, t, part), part)
+        )
+        own_normed = pl.BlockSpec(
+            (tracks, tile, part_width), lambda t, own: (0, own[0] + t, 0)
+        )
+        cross = pl.pallas_call(
+            functools.partial(cross_kernel, groups, part_heads, 1.0 / float(size) ** 0.5),
+            out_shape=(piece_shape,) * (3 * groups),
+            grid_spec=pltpu.PrefetchScalarGridSpec(
+                num_scalar_prefetch=1,
+                grid=(tiles,),
+                in_specs=[bias_spec]
+                + ([own_spec] + [other_spec] * (groups - 1)) * 3
+                + [own_normed]
+                + [result_spec] * (groups - 1),
+                out_specs=(result_spec,) * (3 * groups),
+            ),
+            compiler_params=pltpu.CompilerParams(vmem_limit_bytes=48 * 2**20),
+            cost_estimate=estimate(100),
+        )(own_block, bias, *q_parts, *k_parts, *g_parts, *n_all[part])
+        gn_all.append(returned(cross[:groups]))
+        gq_all.append(returned(cross[groups : 2 * groups]))
+        gk_all.append(returned(cross[2 * groups :]))
+
+    def collect(all_pieces, whole_width):
+        whole = jnp.zeros((tracks, rows, whole_width), BF)
+        for part, pieces in enumerate(all_pieces):
+            for s, piece in enumerate(pieces):
+                start = ((mine + s) % groups) * piece_rows
+                whole = lax.dynamic_update_slice(whole, piece, (0, start, part * part_width))
         return whole
 
-    grad_normed = collect(cross[:groups])
-    grad_cross_query = collect(cross[groups : 2 * groups])
-    grad_cross_key = collect(cross[2 * groups :])
-
-    grad_query, grad_key, grad_value = pl.pallas_call(
-        functools.partial(backward_kernel, count, heads, per),
-        out_shape=(wide,) * 3,
-        in_specs=[vmem] * 8,
-        out_specs=(vmem,) * 3,
-        scratch_shapes=scratch,
-        compiler_params=pltpu.CompilerParams(
-            collective_id=1, has_side_effects=True, vmem_limit_bytes=60 * 2**20
-        ),
-        cost_estimate=pl.CostEstimate(
-            flops=400 * dot_flops, bytes_accessed=16 * slots * size * size, transcendentals=0
-        ),
-        name="backward_chain",
-    )(track_query, track_key, track_value, cols, within, outputs, grad_normed, states)
-    return grad_query, grad_key, grad_value, grad_cross_query, grad_cross_key
+    backward = []
+    for part in range(parts):
+        grad_normed = collect(gn_all[part : part + 1], part_width)
+        backward.append(
+            pl.pallas_call(
+                functools.partial(
+                    backward_kernel, count, part_heads, part * part_heads, heads, per
+                ),
+                out_shape=(narrow,) * 3,
+                grid=(1,),
+                in_specs=[wide_spec(part)] * 3
+                + [col_spec, row_spec, narrow_spec, narrow_spec, state_spec],
+                out_specs=(narrow_spec,) * 3,
+                scratch_shapes=scratch,
+                compiler_params=pltpu.CompilerParams(
+                    collective_id=parts + part,
+                    has_side_effects=True,
+                    vmem_limit_bytes=48 * 2**20,
+                ),
+                cost_estimate=estimate(400),
+            )(
+                track_query,
+                track_key,
+                track_value,
+                cols,
+                within,
+                forward[part][1],
+                grad_normed,
+                forward[part][2],
+            )
+        )
+
+    grads = [
+        jnp.concatenate([backward[part][i] for part in range(parts)], axis=2) for i in range(3)
+    ]
+    return grads[0], grads[1], grads[2], collect(gq_all, width), collect(gk_all, width)
 
 
 def solution(mesh):

time: 334 us -> 292 us (0.87)
  waiting for transfers between devices: 69 us -> 41.7 us
  Pallas kernels: 230 us -> 210 us
  starting transfers between devices: 9.24 us -> 15 us
    ppermute x7 -> x11, waiting for transfers between devices: 69 us -> 41.7 us  [the longest x5 37.4 us: send(): return lax.ppermute(piece, 'track', perm)]
    pallas_call x3 -> x6, Pallas kernels: 230 us -> 210 us  [the longest x2 140 us: per_device(): pl.pallas_call(functools.partial(backward_kernel, count, part_heads, part...]
    ppermute x7 -> x11, starting transfers between devices: 9.24 us -> 15 us  [the longest x6 9.13 us: returned(): lax.ppermute(piece, 'track', back_perms[s])]
    unnamed x37 -> x36, local copies, waits for them, and re-layouts: 13 us -> 7.99 us
    concatenate x0 -> x2, other arithmetic: none -> 4.34 us  [per_device(): jnp.concatenate([backward[part][i] for part in range(parts)], axis=2)]
  transfers between devices with their start and end apart: 7 -> 11, of which waited for: 5 -> 3; matrix products, arithmetic and copies ran while one was open for 2% -> 5% of each run, Pallas kernels for 55% -> 64%
where the time goes in v2:
time: 292 us
  Pallas kernels  210 us (72%)
  waiting for transfers between devices  41.7 us (14%)
  local copies, waits for them, and re-layouts  19 us (7%)
  starting transfers between devices  15 us (5%)
  other arithmetic  5.34 us (2%)
    pallas_call x2, Pallas kernels, per_device(): pl.pallas_call(functools.partial(backward_kernel, count, part_heads, part...  140 us
    pallas_call x2, Pallas kernels, per_device(): pl.pallas_call(functools.partial(forward_kernel, count, part_heads, part...  50.4 us
    ppermute x5, waiting for transfers between devices, send(): return lax.ppermute(piece, 'track', perm)  37.4 us
    pallas_call x2, Pallas kernels, per_device(): pl.pallas_call(functools.partial(cross_kernel, groups, part_heads, 1.0 /...  19.2 us
    ppermute x6, starting transfers between devices, returned(): lax.ppermute(piece, 'track', back_perms[s])  9.13 us
    unnamed x36, local copies, waits for them, and re-layouts  7.99 us
    ppermute x5, starting transfers between devices, send(): return lax.ppermute(piece, 'track', perm)  5.86 us
  transfers between devices with their start and end apart: 11, of which 3 were waited for; matrix products, arithmetic and copies ran while one was open for 5% of the time, Pallas kernels for 64%

profile of v2, /device:TPU:0, one launch (start us, length us, event | category | flops | bytes accessed | tf_op | source)
XLA Modules:
  0.0 292.0 jit_solution(901644769180403118)
XLA Ops:
  2.3 1.6 copy-done.3
  3.8 23.3 %shard_map.128 = (bf16[8,128,512]{2,1,0:T(8,128)(2,1)S(1)}, bf16[8,128,512]{2,1,0:T(8,128)(2,1)S(1)}, bf16[32,128,128]{2,1,0:T(8,128)(2,1)S(1)}) custom-call(bf16[8,128,1024]{2,1,0:T(8,128)(2,1)S(1)} %copy-done.3, bf16[8,128,1024]{2,1,0:T(8,128)(2,1)} %k_ref.7, bf16[8,128,1024]{2,1,0:T(8,128)(2,1)} %v_ref.7, f32[8,128,128]{2,1,0:T(8,128)S(1)} %maximum_maximum_fusion.col_ref, ...), custom_call_target="tpu_custom_call" | custom-call | flops 53687091200 | bytes 8388608 | tf_op jit(solution)/shard_map/pallas_call | solution.py:372
  27.1 1.0 constant_dynamic-slice_fusion.1
  28.1 2.5 collective-permute-start.3
  31.0 1.0 constant_dynamic-slice_fusion.2
  32.6 1.1 copy-done.16
  33.7 1.0 constant_dynamic-slice_fusion.4
  35.3 1.0 constant_dynamic-slice_fusion.3
  36.3 1.5 collective-permute-start.1
  37.8 27.1 %shard_map.131 = (bf16[8,128,512]{2,1,0:T(8,128)(2,1)S(1)}, bf16[8,128,512]{2,1,0:T(8,128)(2,1)S(1)}, bf16[32,128,128]{2,1,0:T(8,128)(2,1)S(1)}) custom-call(bf16[8,128,1024]{2,1,0:T(8,128)(2,1)S(1)} %copy-done.3, bf16[8,128,1024]{2,1,0:T(8,128)(2,1)} %k_ref.7, bf16[8,128,1024]{2,1,0:T(8,128)(2,1)} %v_ref.7, f32[8,128,128]{2,1,0:T(8,128)S(1)} %maximum_maximum_fusion.col_ref, ...), custom_call_target="tpu_custom_call" | custom-call | flops 53687091200 | bytes 8388608 | tf_op jit(solution)/shard_map/pallas_call | solution.py:372
  65.0 1.0 copy-done.7
  65.9 1.0 copy-done.9
  66.9 1.0 constant_dynamic-slice_fusion
  67.9 0.8 collective-permute-start.5
  69.4 15.0 %collective-permute-done.refs_1_ = bf16[8,64,1024]{2,1,0:T(8,128)(2,1)S(1)} collective-permute-done((bf16[8,64,1024]{2,1,0:T(8,128)(2,1)}, bf16[8,64,1024]{2,1,0:T(8,128)(2,1)S(1)}, u32[]{:S(2)}, u32[]{:S(2)}) %collective-permute-start) | collective-permute-done | bytes 1048608 | tf_op jit(solution)/shard_map/ppermute | solution.py:330
  84.4 22.5 %collective-permute-done.1.refs_3_ = bf16[8,64,1024]{2,1,0:T(8,128)(2,1)} collective-permute-done((bf16[8,64,1024]{2,1,0:T(8,128)(2,1)}, bf16[8,64,1024]{2,1,0:T(8,128)(2,1)}, u32[]{:S(2)}, u32[]{:S(2)}) %collective-permute-start.1) | collective-permute-done | bytes 1048608 | tf_op jit(solution)/shard_map/ppermute | solution.py:330
  106.8 9.6 %shard_map.129 = (bf16[8,64,512]{2,1,0:T(8,128)(2,1)S(1)}, bf16[8,64,512]{2,1,0:T(8,128)(2,1)S(1)}, bf16[8,64,512]{2,1,0:T(8,128)(2,1)S(1)}, bf16[8,64,512]{2,1,...) custom-call(s32[1]{0:T(128)} %bitcast.4.own_ref, ...), custom_call_target="tpu_custom_call" | custom-call | flops 13421772800 | bytes 8388608 | tf_op jit(solution)/shard_map/pallas_call | solution.py:430
  116.4 2.5 collective-permute-start.9
  119.0 9.6 %shard_map.132 = (bf16[8,64,512]{2,1,0:T(8,128)(2,1)S(1)}, bf16[8,64,512]{2,1,0:T(8,128)(2,1)S(1)}, bf16[8,64,512]{2,1,0:T(8,128)(2,1)S(1)}, bf16[8,64,512]{2,1,...) custom-call(s32[1]{0:T(128)} %bitcast.4.own_ref, ...), custom_call_target="tpu_custom_call" | custom-call | flops 13421772800 | bytes 8388608 | tf_op jit(solution)/shard_map/pallas_call | solution.py:430
  128.7 2.0 collective-permute-start.10
  130.7 1.9 collective-permute-start.8
  133.4 1.3 copy-done.12
  135.0 4.2 %collective-permute-done.4 = bf16[8,64,512]{2,1,0:T(8,128)(2,1)S(1)} collective-permute-done((bf16[8,64,512]{2,1,0:T(8,128)(2,1)S(1)}, bf16[8,64,512]{2,1,0:T(8,128)(2,1)S(1)}, u32[]{:S(2)}, u32[]{:S(2)}) %collective-permute-start.4) | collective-permute-done | bytes 524320 | tf_op jit(solution)/shard_map/ppermute | solution.py:409
  139.2 2.5 collective-permute-start.6
  141.8 98.0 %shard_map.130 = (bf16[8,128,512]{2,1,0:T(8,128)(2,1)S(1)}, bf16[8,128,512]{2,1,0:T(8,128)(2,1)S(1)}, bf16[8,128,512]{2,1,0:T(8,128)(2,1)S(1)}) custom-call(bf16[8,128,1024]{2,1,0:T(8,128)(2,1)} %q_ref.7, bf16[8,128,1024]{2,1,0:T(8,128)(2,1)} %k_ref.7, bf16[8,128,1024]{2,1,0:T(8,128)(2,1)} %v_ref.7, f32[8,128,128]{2,1,0:T(8,128)S(1)} %maximum_maximum_fusion.col_ref, ...), custom_call_target="tpu_custom_call" | custom-call | flops 53687091200 | bytes 8388608 | tf_op jit(solution)/shard_map/pallas_call | solution.py:461
  239.9 42.1 %shard_map.133 = (bf16[8,128,512]{2,1,0:T(8,128)(2,1)S(1)}, bf16[8,128,512]{2,1,0:T(8,128)(2,1)S(1)}, bf16[8,128,512]{2,1,0:T(8,128)(2,1)S(1)}) custom-call(bf16[8,128,1024]{2,1,0:T(8,128)(2,1)} %q_ref.7, bf16[8,128,1024]{2,1,0:T(8,128)(2,1)} %k_ref.7, bf16[8,128,1024]{2,1,0:T(8,128)(2,1)} %v_ref.7, f32[8,128,128]{2,1,0:T(8,128)S(1)} %maximum_maximum_fusion.col_ref, ...), custom_call_target="tpu_custom_call" | custom-call | flops 53687091200 | bytes 8388608 | tf_op jit(solution)/shard_map/pallas_call | solution.py:461
  282.0 1.2 constant_dynamic-update-slice_fusion.2
  283.8 1.1 constant_dynamic-update-slice_fusion.6
  285.0 1.1 constant_dynamic-update-slice_fusion
  286.1 1.8 pad_maximum_fusion.2
  288.1 2.6 pad_maximum_fusion
  290.7 1.3 copy-done.14
  (76 shorter events, 5.6 us)
Async XLA Ops:
  0.6 0.8 copy-start
  2.2 1.6 copy-start.3
  3.8 26.9 %copy-start.15 = (bf16[8,128,1024]{2,1,0:T(8,128)(2,1)S(1)}, bf16[8,128,1024]{2,1,0:T(8,128)(2,1)}, u32[]{:S(2)}) copy-start(bf16[8,128,1024]{2,1,0:T(8,128)(2,1)} %param.17) | copy-start | bytes 6291460
  27.1 3.8 %copy-start.1 = (bf16[8,128,512]{2,1,0:T(8,128)(2,1)}, bf16[8,128,512]{2,1,0:T(8,128)(2,1)S(1)}, u32[]{:S(2)}) copy-start(bf16[8,128,512]{2,1,0:T(8,128)(2,1)S(1)} %get-tuple-element.30.refs_6_) | copy-start | bytes 3145732
  27.1 3.8 %copy-start.4 = (bf16[8,128,512]{2,1,0:T(8,128)(2,1)}, bf16[8,128,512]{2,1,0:T(8,128)(2,1)S(1)}, u32[]{:S(2)}) copy-start(bf16[8,128,512]{2,1,0:T(8,128)(2,1)S(1)} %get-tuple-element.29.out_ref) | copy-start | bytes 3145732
  27.1 3.8 %copy-start.6 = (bf16[32,128,128]{2,1,0:T(8,128)(2,1)}, bf16[32,128,128]{2,1,0:T(8,128)(2,1)S(1)}, u32[]{:S(2)}) copy-start(bf16[32,128,128]{2,1,0:T(8,128)(2,1)S(1)} %get-tuple-element.33.state_ref) | copy-start | bytes 3145732
  28.1 41.3 %collective-permute-start.3 = (bf16[8,64,512]{2,1,0:T(8,128)(2,1)}, bf16[8,64,512]{2,1,0:T(8,128)(2,1)S(1)}, u32[]{:S(2)}, u32[]{:S(2)}) collective-permute-start(bf16[8,64,512]{2,1,0:T(8,128)(2,1)} %constant_dynamic-slice_fusion.1), channel_id=1, source_target_pairs={{0,16},{16,0},{1,17},{17,1},{2,18},{18,2},{3,19},{19,3},{4,20},{20... | collective-permute-start | bytes 1572872 | tf_op jit(solution)/shard_map/ppermute | solution.py:330
  31.0 3.8 %copy-start.10 = (bf16[8,128,1024]{2,1,0:T(8,128)(2,1)}, bf16[8,128,1024]{2,1,0:T(8,128)(2,1)S(1)}, u32[]{:S(2)}) copy-start(bf16[8,128,1024]{2,1,0:T(8,128)(2,1)S(1)} %broadcast_multiply_fusion.refs_4_) | copy-start | bytes 6291460
  31.0 2.7 copy-start.16
  31.0 4.3 %copy-start.17 = (bf16[8,128,1024]{2,1,0:T(8,128)(2,1)S(1)}, bf16[8,128,1024]{2,1,0:T(8,128)(2,1)}, u32[]{:S(2)}) copy-start(bf16[8,128,1024]{2,1,0:T(8,128)(2,1)} %refs_2_.3) | copy-start | bytes 6291460
  32.0 37.4 %collective-permute-start.2 = (bf16[8,64,1024]{2,1,0:T(8,128)(2,1)}, bf16[8,64,1024]{2,1,0:T(8,128)(2,1)}, u32[]{:S(2)}, u32[]{:S(2)}) collective-permute-start(bf16[8,64,1024]{2,1,0:T(8,128)(2,1)} %constant_dynamic-slice_fusion.2), channel_id=1, source_target_pairs={{0,16},{16,0},{1,17},{17,1},{2,18},{18,2},{3,19},{19,3},{4,20},{20... | collective-permute-start | bytes 3145736 | tf_op jit(solution)/shard_map/ppermute | solution.py:330
  34.7 49.6 %collective-permute-start = (bf16[8,64,1024]{2,1,0:T(8,128)(2,1)}, bf16[8,64,1024]{2,1,0:T(8,128)(2,1)S(1)}, u32[]{:S(2)}, u32[]{:S(2)}) collective-permute-start(bf16[8,64,1024]{2,1,0:T(8,128)(2,1)} %constant_dynamic-slice_fusion.4), channel_id=1, source_target_pairs={{0,16},{16,0},{1,17},{17,1},{2,18},{18,2},{3,19},{19,3},{4,20},{20... | collective-permute-start | bytes 3145736 | tf_op jit(solution)/shard_map/ppermute | solution.py:330
  36.3 70.5 %collective-permute-start.1 = (bf16[8,64,1024]{2,1,0:T(8,128)(2,1)}, bf16[8,64,1024]{2,1,0:T(8,128)(2,1)}, u32[]{:S(2)}, u32[]{:S(2)}) collective-permute-start(bf16[8,64,1024]{2,1,0:T(8,128)(2,1)} %constant_dynamic-slice_fusion.3), channel_id=1, source_target_pairs={{0,16},{16,0},{1,17},{17,1},{2,18},{18,2},{3,19},{19,3},{4,20},{20... | collective-permute-start | bytes 3145736 | tf_op jit(solution)/shard_map/ppermute | solution.py:330
  65.0 1.0 copy-start.7
  65.9 1.0 copy-start.9
  66.9 49.5 %copy-start.2 = (bf16[8,128,512]{2,1,0:T(8,128)(2,1)}, bf16[8,128,512]{2,1,0:T(8,128)(2,1)S(1)}, u32[]{:S(2)}) copy-start(bf16[8,128,512]{2,1,0:T(8,128)(2,1)S(1)} %get-tuple-element.36.refs_6_) | copy-start | bytes 3145732
  67.9 51.2 %collective-permute-start.5 = (bf16[8,64,512]{2,1,0:T(8,128)(2,1)}, bf16[8,64,512]{2,1,0:T(8,128)(2,1)}, u32[]{:S(2)}, u32[]{:S(2)}) collective-permute-start(bf16[8,64,512]{2,1,0:T(8,128)(2,1)} %constant_dynamic-slice_fusion), channel_id=1, source_target_pairs={{0,16},{16,0},{1,17},{17,1},{2,18},{18,2},{3,19},{19,3},{4,20},{20... | collective-permute-start | bytes 1572872 | tf_op jit(solution)/shard_map/ppermute | solution.py:330
  116.4 165.6 %collective-permute-start.9 = (bf16[8,64,512]{2,1,0:T(8,128)(2,1)S(1)}, bf16[8,64,512]{2,1,0:T(8,128)(2,1)}, u32[]{:S(2)}, u32[]{:S(2)}) collective-permute-start(bf16[8,64,512]{2,1,0:T(8,128)(2,1)S(1)} %get-tuple-element.50), channel_id=1, source_target_pairs={{0,16},{16,0},{1,17},{17,1},{2,18},{18,2},{3,19},{19,3},{4,20},{20... | collective-permute-start | bytes 1572872 | tf_op jit(solution)/shard_map/ppermute | solution.py:409
  119.0 20.3 %collective-permute-start.4 = (bf16[8,64,512]{2,1,0:T(8,128)(2,1)S(1)}, bf16[8,64,512]{2,1,0:T(8,128)(2,1)S(1)}, u32[]{:S(2)}, u32[]{:S(2)}) collective-permute-start(bf16[8,64,512]{2,1,0:T(8,128)(2,1)S(1)} %get-tuple-element.32), channel_id=1, source_target_pairs={{0,16},{16,0},{1,17},{17,1},{2,18},{18,2},{3,19},{19,3},{4,20},{20... | collective-permute-start | bytes 1572872 | tf_op jit(solution)/shard_map/ppermute | solution.py:409
  128.7 156.3 %collective-permute-start.10 = (bf16[8,64,512]{2,1,0:T(8,128)(2,1)S(1)}, bf16[8,64,512]{2,1,0:T(8,128)(2,1)}, u32[]{:S(2)}, u32[]{:S(2)}) collective-permute-start(bf16[8,64,512]{2,1,0:T(8,128)(2,1)S(1)} %get-tuple-element.52), channel_id=1, source_target_pairs={{0,16},{16,0},{1,17},{17,1},{2,18},{18,2},{3,19},{19,3},{4,20},{20... | collective-permute-start | bytes 1572872 | tf_op jit(solution)/shard_map/ppermute | solution.py:409
  130.7 152.7 %collective-permute-start.7 = (bf16[8,64,512]{2,1,0:T(8,128)(2,1)S(1)}, bf16[8,64,512]{2,1,0:T(8,128)(2,1)}, u32[]{:S(2)}, u32[]{:S(2)}) collective-permute-start(bf16[8,64,512]{2,1,0:T(8,128)(2,1)S(1)} %get-tuple-element.46), channel_id=1, source_target_pairs={{0,16},{16,0},{1,17},{17,1},{2,18},{18,2},{3,19},{19,3},{4,20},{20... | collective-permute-start | bytes 1572872 | tf_op jit(solution)/shard_map/ppermute | solution.py:409
  130.7 159.9 %collective-permute-start.8 = (bf16[8,64,512]{2,1,0:T(8,128)(2,1)S(1)}, bf16[8,64,512]{2,1,0:T(8,128)(2,1)S(1)}, u32[]{:S(2)}, u32[]{:S(2)}) collective-permute-start(bf16[8,64,512]{2,1,0:T(8,128)(2,1)S(1)} %get-tuple-element.48), channel_id=1, source_target_pairs={{0,16},{16,0},{1,17},{17,1},{2,18},{18,2},{3,19},{19,3},{4,20},{20... | collective-permute-start | bytes 1572872 | tf_op jit(solution)/shard_map/ppermute | solution.py:409
  133.4 1.3 copy-start.12
  134.8 7.0 %copy-start.5 = (bf16[8,128,512]{2,1,0:T(8,128)(2,1)S(1)}, bf16[8,128,512]{2,1,0:T(8,128)(2,1)}, u32[]{:S(2)}) copy-start(bf16[8,128,512]{2,1,0:T(8,128)(2,1)} %copy-done.4) | copy-start | bytes 3145732
  139.2 100.6 %collective-permute-start.6 = (bf16[8,64,512]{2,1,0:T(8,128)(2,1)S(1)}, bf16[8,64,512]{2,1,0:T(8,128)(2,1)S(1)}, u32[]{:S(2)}, u32[]{:S(2)}) collective-permute-start(bf16[8,64,512]{2,1,0:T(8,128)(2,1)S(1)} %get-tuple-element.38), channel_id=1, source_target_pairs={{0,16},{16,0},{1,17},{17,1},{2,18},{18,2},{3,19},{19,3},{4,20},{20... | collective-permute-start | bytes 1572872 | tf_op jit(solution)/shard_map/ppermute | solution.py:409
  141.8 98.1 %copy-start.8 = (bf16[8,128,512]{2,1,0:T(8,128)(2,1)S(1)}, bf16[8,128,512]{2,1,0:T(8,128)(2,1)}, u32[]{:S(2)}) copy-start(bf16[8,128,512]{2,1,0:T(8,128)(2,1)} %copy-done.7) | copy-start | bytes 3145732
  282.0 1.8 copy-start.13
  286.1 2.0 copy-start.11
  290.7 1.3 copy-start.14

commit v3 on v2

--- a/solution.py
+++ b/solution.py
@@ -379,7 +379,7 @@
                 compiler_params=pltpu.CompilerParams(
                     collective_id=part,
                     has_side_effects=True,
-                    vmem_limit_bytes=48 * 2**20,
+                    vmem_limit_bytes=63 * 2**20,
                 ),
                 cost_estimate=estimate(400),
             )(track_query, track_key, track_value, cols, within, initial_state)
@@ -439,7 +439,7 @@
                 + [result_spec] * (groups - 1),
                 out_specs=(result_spec,) * (3 * groups),
             ),
-            compiler_params=pltpu.CompilerParams(vmem_limit_bytes=48 * 2**20),
+            compiler_params=pltpu.CompilerParams(vmem_limit_bytes=63 * 2**20),
             cost_estimate=estimate(100),
         )(own_block, bias, *q_parts, *k_parts, *g_parts, *n_all[part])
         gn_all.append(returned(cross[:groups]))
@@ -471,7 +471,7 @@
                 compiler_params=pltpu.CompilerParams(
                     collective_id=parts + part,
                     has_side_effects=True,
-                    vmem_limit_bytes=48 * 2**20,
+                    vmem_limit_bytes=63 * 2**20,
                 ),
                 cost_estimate=estimate(400),
             )(

time: 292 us -> 304 us (1.041)
  local copies, waits for them, and re-layouts: 19 us -> 28 us
  Pallas kernels: 210 us -> 218 us
  waiting for transfers between devices: 41.7 us -> 34.8 us
  other arithmetic: 5.34 us -> 8.5 us
    dynamic_update_slice x12, local copies, waits for them, and re-layouts: 3.98 us -> 12.7 us  [collect(): lax.dynamic_update_slice(whole, piece, (0, start, part * part_width))]
    ppermute x6, waiting for transfers between devices: 4.24 us -> 0.02 us  [returned(): lax.ppermute(piece, 'track', back_perms[s])]
    pallas_call x2, Pallas kernels: 50.4 us -> 54.4 us  [per_device(): pl.pallas_call(functools.partial(forward_kernel, count, part_heads, part...]
    unnamed x36 -> x40, local copies, waits for them, and re-layouts: 7.99 us -> 5.13 us
  transfers between devices with their start and end apart: 11 -> 11, of which waited for: 3 -> 2; matrix products, arithmetic and copies ran while one was open for 5% -> 9% of each run, Pallas kernels for 64% -> 64%
where the time goes in v3:
time: 304 us; the launch traced here: 303 us
  Pallas kernels  218 us (72%)
  waiting for transfers between devices  34.8 us (11%)
  local copies, waits for them, and re-layouts  28 us (9%)
  starting transfers between devices  12.8 us (4%)
  other arithmetic  8.5 us (3%)
    pallas_call x2, Pallas kernels, per_device(): pl.pallas_call(functools.partial(backward_kernel, count, part_heads, part...  143 us
    pallas_call x2, Pallas kernels, per_device(): pl.pallas_call(functools.partial(forward_kernel, count, part_heads, part...  54.4 us
    ppermute x5, waiting for transfers between devices, send(): return lax.ppermute(piece, 'track', perm)  34.8 us
    pallas_call x2, Pallas kernels, per_device(): pl.pallas_call(functools.partial(cross_kernel, groups, part_heads, 1.0 /...  20.8 us
    dynamic_update_slice x12, local copies, waits for them, and re-layouts, collect(): lax.dynamic_update_slice(whole, piece, (0, start, part * part_width))  12.7 us
    ppermute x6, starting transfers between devices, returned(): lax.ppermute(piece, 'track', back_perms[s])  7.68 us
    dynamic_slice x5, local copies, waits for them, and re-layouts, send(): piece = lax.dynamic_slice_in_dim(value, start, piece_rows, axis=1)  6.21 us
  transfers between devices with their start and end apart: 11, of which 2 were waited for; matrix products, arithmetic and copies ran while one was open for 9% of the time, Pallas kernels for 64%

profile of v3, /device:TPU:0, one launch (start us, length us, event | category | flops | bytes accessed | tf_op | source)
XLA Modules:
  0.0 303.5 jit_solution(7930299133761935190)
XLA Ops:
  3.1 25.2 %shard_map.128 = (bf16[8,128,512]{2,1,0:T(8,128)(2,1)}, bf16[8,128,512]{2,1,0:T(8,128)(2,1)}, bf16[32,128,128]{2,1,0:T(8,128)(2,1)}) custom-call(bf16[8,128,1024]{2,1,0:T(8,128)(2,1)} %q_ref.7, bf16[8,128,1024]{2,1,0:T(8,128)(2,1)} %k_ref.7, bf16[8,128,1024]{2,1,0:T(8,128)(2,1)} %v_ref.7, f32[8,128,128]{2,1,0:T(8,128)} %maximum_maximum_fusion.col_ref, ...), custom_call_target="tpu_custom_call" | custom-call | flops 53687091200 | bytes 8388608 | tf_op jit(solution)/shard_map/pallas_call | solution.py:372
  28.3 1.9 constant_dynamic-slice_fusion.1
  30.1 2.5 collective-permute-start.3
  32.7 1.8 broadcast_multiply_fusion.refs_4_
  34.6 1.1 constant_dynamic-slice_fusion.2
  35.6 1.6 copy-done.12
  37.3 1.1 constant_dynamic-slice_fusion.4
  38.8 1.1 constant_dynamic-slice_fusion.3
  39.8 1.6 collective-permute-start.1
  41.5 29.2 %shard_map.131 = (bf16[8,128,512]{2,1,0:T(8,128)(2,1)}, bf16[8,128,512]{2,1,0:T(8,128)(2,1)}, bf16[32,128,128]{2,1,0:T(8,128)(2,1)}) custom-call(bf16[8,128,1024]{2,1,0:T(8,128)(2,1)} %q_ref.7, bf16[8,128,1024]{2,1,0:T(8,128)(2,1)} %k_ref.7, bf16[8,128,1024]{2,1,0:T(8,128)(2,1)} %v_ref.7, f32[8,128,128]{2,1,0:T(8,128)} %maximum_maximum_fusion.col_ref, ...), custom_call_target="tpu_custom_call" | custom-call | flops 53687091200 | bytes 8388608 | tf_op jit(solution)/shard_map/pallas_call | solution.py:372
  70.7 1.1 constant_dynamic-slice_fusion
  72.8 1.2 and_select_fusion.bias_ref
  74.0 12.4 %collective-permute-done.refs_1_ = bf16[8,64,1024]{2,1,0:T(8,128)(2,1)} collective-permute-done((bf16[8,64,1024]{2,1,0:T(8,128)(2,1)}, bf16[8,64,1024]{2,1,0:T(8,128)(2,1)}, u32[]{:S(2)}, u32[]{:S(2)}) %collective-permute-start) | collective-permute-done | bytes 1048608 | tf_op jit(solution)/shard_map/ppermute | solution.py:330
  86.3 22.5 %collective-permute-done.1.refs_3_ = bf16[8,64,1024]{2,1,0:T(8,128)(2,1)} collective-permute-done((bf16[8,64,1024]{2,1,0:T(8,128)(2,1)}, bf16[8,64,1024]{2,1,0:T(8,128)(2,1)}, u32[]{:S(2)}, u32[]{:S(2)}) %collective-permute-start.1) | collective-permute-done | bytes 1048608 | tf_op jit(solution)/shard_map/ppermute | solution.py:330
  108.8 10.4 %shard_map.129 = (bf16[8,64,512]{2,1,0:T(8,128)(2,1)}, bf16[8,64,512]{2,1,0:T(8,128)(2,1)}, bf16[8,64,512]{2,1,0:T(8,128)(2,1)}, bf16[8,64,512]{2,1,0:T(8,128)(2...) custom-call(s32[1]{0:T(128)} %bitcast.4.own_ref, f32[4,256,256]{2,1,0:T(8,128)} %and_select_fusion.bias_ref, ...), custom_call_target="tpu_custom_call" | custom-call | flops 13421772800 | bytes 8388608 | tf_op jit(solution)/shard_map/pallas_call | solution.py:430
  119.2 2.6 collective-permute-start.9
  121.9 10.4 %shard_map.132 = (bf16[8,64,512]{2,1,0:T(8,128)(2,1)}, bf16[8,64,512]{2,1,0:T(8,128)(2,1)}, bf16[8,64,512]{2,1,0:T(8,128)(2,1)}, bf16[8,64,512]{2,1,0:T(8,128)(2...) custom-call(s32[1]{0:T(128)} %bitcast.4.own_ref, f32[4,256,256]{2,1,0:T(8,128)} %and_select_fusion.bias_ref, ...), custom_call_target="tpu_custom_call" | custom-call | flops 13421772800 | bytes 8388608 | tf_op jit(solution)/shard_map/pallas_call | solution.py:430
  132.3 2.0 collective-permute-start.10
  134.4 1.9 collective-permute-start.8
  137.9 1.1 broadcast.152.clone.1
  139.8 1.1 broadcast.152.clone
  142.7 1.9 constant_dynamic-update-slice_fusion.10.gn_ref
  144.6 102.6 %shard_map.130 = (bf16[8,128,512]{2,1,0:T(8,128)(2,1)}, bf16[8,128,512]{2,1,0:T(8,128)(2,1)}, bf16[8,128,512]{2,1,0:T(8,128)(2,1)}) custom-call(bf16[8,128,1024]{2,1,0:T(8,128)(2,1)} %q_ref.7, bf16[8,128,1024]{2,1,0:T(8,128)(2,1)} %k_ref.7, bf16[8,128,1024]{2,1,0:T(8,128)(2,1)} %v_ref.7, f32[8,128,128]{2,1,0:T(8,128)} %maximum_maximum_fusion.col_ref, ...), custom_call_target="tpu_custom_call" | custom-call | flops 53687091200 | bytes 8388608 | tf_op jit(solution)/shard_map/pallas_call | solution.py:461
  247.2 1.9 constant_dynamic-update-slice_fusion.8.gn_ref
  249.1 40.3 %shard_map.133 = (bf16[8,128,512]{2,1,0:T(8,128)(2,1)}, bf16[8,128,512]{2,1,0:T(8,128)(2,1)}, bf16[8,128,512]{2,1,0:T(8,128)(2,1)}) custom-call(bf16[8,128,1024]{2,1,0:T(8,128)(2,1)} %q_ref.7, bf16[8,128,1024]{2,1,0:T(8,128)(2,1)} %k_ref.7, bf16[8,128,1024]{2,1,0:T(8,128)(2,1)} %v_ref.7, f32[8,128,128]{2,1,0:T(8,128)} %maximum_maximum_fusion.col_ref, ...), custom_call_target="tpu_custom_call" | custom-call | flops 53687091200 | bytes 8388608 | tf_op jit(solution)/shard_map/pallas_call | solution.py:461
  289.4 2.0 constant_dynamic-update-slice_fusion.2
  291.5 2.0 constant_dynamic-update-slice_fusion.1
  293.5 1.1 constant_dynamic-update-slice_fusion.6
  294.7 1.9 constant_dynamic-update-slice_fusion
  296.6 1.6 pad_maximum_fusion.2
  299.5 2.6 pad_maximum_fusion
  302.1 1.3 copy-done.5
  (80 shorter events, 9.7 us)
Async XLA Ops:
  0.6 0.8 copy-start
  1.6 1.5 copy-start.19
  30.1 43.8 %collective-permute-start.3 = (bf16[8,64,512]{2,1,0:T(8,128)(2,1)}, bf16[8,64,512]{2,1,0:T(8,128)(2,1)}, u32[]{:S(2)}, u32[]{:S(2)}) collective-permute-start(bf16[8,64,512]{2,1,0:T(8,128)(2,1)} %constant_dynamic-slice_fusion.1), channel_id=1, source_target_pairs={{0,16},{16,0},{1,17},{17,1},{2,18},{18,2},{3,19},{19,3},{4,20},{20... | collective-permute-start | bytes 1572872 | tf_op jit(solution)/shard_map/ppermute | solution.py:330
  34.5 3.8 %copy-start.1 = (bf16[8,128,1024]{2,1,0:T(8,128)(2,1)}, bf16[8,128,1024]{2,1,0:T(8,128)(2,1)S(1)}, u32[]{:S(2)}) copy-start(bf16[8,128,1024]{2,1,0:T(8,128)(2,1)S(1)} %broadcast_multiply_fusion.refs_4_) | copy-start | bytes 6291460
  34.5 2.7 copy-start.12
  34.5 4.2 %copy-start.13 = (bf16[8,128,1024]{2,1,0:T(8,128)(2,1)S(1)}, bf16[8,128,1024]{2,1,0:T(8,128)(2,1)}, u32[]{:S(2)}) copy-start(bf16[8,128,1024]{2,1,0:T(8,128)(2,1)} %refs_2_.3) | copy-start | bytes 6291460
  35.6 38.3 %collective-permute-start.2 = (bf16[8,64,1024]{2,1,0:T(8,128)(2,1)}, bf16[8,64,1024]{2,1,0:T(8,128)(2,1)}, u32[]{:S(2)}, u32[]{:S(2)}) collective-permute-start(bf16[8,64,1024]{2,1,0:T(8,128)(2,1)} %constant_dynamic-slice_fusion.2), channel_id=1, source_target_pairs={{0,16},{16,0},{1,17},{17,1},{2,18},{18,2},{3,19},{19,3},{4,20},{20... | collective-permute-start | bytes 3145736 | tf_op jit(solution)/shard_map/ppermute | solution.py:330
  38.3 48.0 %collective-permute-start = (bf16[8,64,1024]{2,1,0:T(8,128)(2,1)}, bf16[8,64,1024]{2,1,0:T(8,128)(2,1)}, u32[]{:S(2)}, u32[]{:S(2)}) collective-permute-start(bf16[8,64,1024]{2,1,0:T(8,128)(2,1)} %constant_dynamic-slice_fusion.4), channel_id=1, source_target_pairs={{0,16},{16,0},{1,17},{17,1},{2,18},{18,2},{3,19},{19,3},{4,20},{20... | collective-permute-start | bytes 3145736 | tf_op jit(solution)/shard_map/ppermute | solution.py:330
  39.8 69.0 %collective-permute-start.1 = (bf16[8,64,1024]{2,1,0:T(8,128)(2,1)}, bf16[8,64,1024]{2,1,0:T(8,128)(2,1)}, u32[]{:S(2)}, u32[]{:S(2)}) collective-permute-start(bf16[8,64,1024]{2,1,0:T(8,128)(2,1)} %constant_dynamic-slice_fusion.3), channel_id=1, source_target_pairs={{0,16},{16,0},{1,17},{17,1},{2,18},{18,2},{3,19},{19,3},{4,20},{20... | collective-permute-start | bytes 3145736 | tf_op jit(solution)/shard_map/ppermute | solution.py:330
  71.8 50.1 %collective-permute-start.5 = (bf16[8,64,512]{2,1,0:T(8,128)(2,1)S(1)}, bf16[8,64,512]{2,1,0:T(8,128)(2,1)}, u32[]{:S(2)}, u32[]{:S(2)}) collective-permute-start(bf16[8,64,512]{2,1,0:T(8,128)(2,1)S(1)} %constant_dynamic-slice_fusion), channel_id=1, source_target_pairs={{0,16},{16,0},{1,17},{17,1},{2,18},{18,2},{3,19},{19,3},{4,20},{20... | collective-permute-start | bytes 1572872 | tf_op jit(solution)/shard_map/ppermute | solution.py:330
  119.2 170.2 %collective-permute-start.9 = (bf16[8,64,512]{2,1,0:T(8,128)(2,1)}, bf16[8,64,512]{2,1,0:T(8,128)(2,1)}, u32[]{:S(2)}, u32[]{:S(2)}) collective-permute-start(bf16[8,64,512]{2,1,0:T(8,128)(2,1)} %get-tuple-element.50), channel_id=1, source_target_pairs={{0,16},{16,0},{1,17},{17,1},{2,18},{18,2},{3,19},{19,3},{4,20},{20... | collective-permute-start | bytes 1572872 | tf_op jit(solution)/shard_map/ppermute | solution.py:409
  121.8 19.9 %collective-permute-start.4 = (bf16[8,64,512]{2,1,0:T(8,128)(2,1)}, bf16[8,64,512]{2,1,0:T(8,128)(2,1)}, u32[]{:S(2)}, u32[]{:S(2)}) collective-permute-start(bf16[8,64,512]{2,1,0:T(8,128)(2,1)} %get-tuple-element.32), channel_id=1, source_target_pairs={{0,16},{16,0},{1,17},{17,1},{2,18},{18,2},{3,19},{19,3},{4,20},{20... | collective-permute-start | bytes 1572872 | tf_op jit(solution)/shard_map/ppermute | solution.py:409
  132.3 4.3 %copy-start.17 = (bf16[8,64,512]{2,1,0:T(8,128)(2,1)S(1)}, bf16[8,64,512]{2,1,0:T(8,128)(2,1)}, u32[]{:S(2)}) copy-start(bf16[8,64,512]{2,1,0:T(8,128)(2,1)} %get-tuple-element.49) | copy-start | bytes 1572868
  132.3 162.4 %collective-permute-start.10 = (bf16[8,64,512]{2,1,0:T(8,128)(2,1)}, bf16[8,64,512]{2,1,0:T(8,128)(2,1)}, u32[]{:S(2)}, u32[]{:S(2)}) collective-permute-start(bf16[8,64,512]{2,1,0:T(8,128)(2,1)} %get-tuple-element.52), channel_id=1, source_target_pairs={{0,16},{16,0},{1,17},{17,1},{2,18},{18,2},{3,19},{19,3},{4,20},{20... | collective-permute-start | bytes 1572872 | tf_op jit(solution)/shard_map/ppermute | solution.py:409
  134.3 159.1 %collective-permute-start.7 = (bf16[8,64,512]{2,1,0:T(8,128)(2,1)}, bf16[8,64,512]{2,1,0:T(8,128)(2,1)}, u32[]{:S(2)}, u32[]{:S(2)}) collective-permute-start(bf16[8,64,512]{2,1,0:T(8,128)(2,1)} %get-tuple-element.46), channel_id=1, source_target_pairs={{0,16},{16,0},{1,17},{17,1},{2,18},{18,2},{3,19},{19,3},{4,20},{20... | collective-permute-start | bytes 1572872 | tf_op jit(solution)/shard_map/ppermute | solution.py:409
  134.4 167.6 %collective-permute-start.8 = (bf16[8,64,512]{2,1,0:T(8,128)(2,1)}, bf16[8,64,512]{2,1,0:T(8,128)(2,1)S(1)}, u32[]{:S(2)}, u32[]{:S(2)}) collective-permute-start(bf16[8,64,512]{2,1,0:T(8,128)(2,1)} %get-tuple-element.48), channel_id=1, source_target_pairs={{0,16},{16,0},{1,17},{17,1},{2,18},{18,2},{3,19},{19,3},{4,20},{20... | collective-permute-start | bytes 1572872 | tf_op jit(solution)/shard_map/ppermute | solution.py:409
  136.6 1.2 copy-start.16
  136.7 2.2 copy-start.2
  136.7 2.2 copy-start.15
  137.8 3.1 %copy-start.18 = (bf16[8,64,512]{2,1,0:T(8,128)(2,1)S(1)}, bf16[8,64,512]{2,1,0:T(8,128)(2,1)}, u32[]{:S(2)}) copy-start(bf16[8,64,512]{2,1,0:T(8,128)(2,1)} %get-tuple-element.37) | copy-start | bytes 1572868
  137.9 2.0 copy-start.3
  141.7 105.5 %collective-permute-start.6 = (bf16[8,64,512]{2,1,0:T(8,128)(2,1)}, bf16[8,64,512]{2,1,0:T(8,128)(2,1)}, u32[]{:S(2)}, u32[]{:S(2)}) collective-permute-start(bf16[8,64,512]{2,1,0:T(8,128)(2,1)} %get-tuple-element.38), channel_id=1, source_target_pairs={{0,16},{16,0},{1,17},{17,1},{2,18},{18,2},{3,19},{19,3},{4,20},{20... | collective-permute-start | bytes 1572872 | tf_op jit(solution)/shard_map/ppermute | solution.py:409
  289.4 4.1 %copy-start.4 = (bf16[8,128,1024]{2,1,0:T(8,128)(2,1)S(1)}, bf16[8,128,1024]{2,1,0:T(8,128)(2,1)}, u32[]{:S(2)}) copy-start(bf16[8,128,1024]{2,1,0:T(8,128)(2,1)} %copy-done.3) | copy-start | bytes 6291460
  289.4 5.2 %copy-start.14 = (bf16[8,64,512]{2,1,0:T(8,128)(2,1)S(1)}, bf16[8,64,512]{2,1,0:T(8,128)(2,1)}, u32[]{:S(2)}) copy-start(bf16[8,64,512]{2,1,0:T(8,128)(2,1)} %get-tuple-element.47) | copy-start | bytes 1572868
  291.5 5.1 %copy-start.6 = (bf16[8,128,512]{2,1,0:T(8,128)(2,1)S(1)}, bf16[8,128,512]{2,1,0:T(8,128)(2,1)}, u32[]{:S(2)}) copy-start(bf16[8,128,512]{2,1,0:T(8,128)(2,1)} %get-tuple-element.43) | copy-start | bytes 3145732
  291.5 5.1 %copy-start.7 = (bf16[8,128,512]{2,1,0:T(8,128)(2,1)S(1)}, bf16[8,128,512]{2,1,0:T(8,128)(2,1)}, u32[]{:S(2)}) copy-start(bf16[8,128,512]{2,1,0:T(8,128)(2,1)} %get-tuple-element.44) | copy-start | bytes 3145732
  296.6 1.6 copy-start.8
  296.6 2.3 copy-start.9
  296.6 2.6 copy-start.10
  296.6 2.9 copy-start.11
  302.1 1.3 copy-start.5

commit v4 on v3

--- a/solution.py
+++ b/solution.py
@@ -379,7 +379,7 @@
                 compiler_params=pltpu.CompilerParams(
                     collective_id=part,
                     has_side_effects=True,
-                    vmem_limit_bytes=63 * 2**20,
+                    vmem_limit_bytes=28 * 2**20,
                 ),
                 cost_estimate=estimate(400),
             )(track_query, track_key, track_value, cols, within, initial_state)
@@ -439,7 +439,7 @@
                 + [result_spec] * (groups - 1),
                 out_specs=(result_spec,) * (3 * groups),
             ),
-            compiler_params=pltpu.CompilerParams(vmem_limit_bytes=63 * 2**20),
+            compiler_params=pltpu.CompilerParams(vmem_limit_bytes=28 * 2**20),
             cost_estimate=estimate(100),
         )(own_block, bias, *q_parts, *k_parts, *g_parts, *n_all[part])
         gn_all.append(returned(cross[:groups]))
@@ -471,7 +471,7 @@
                 compiler_params=pltpu.CompilerParams(
                     collective_id=parts + part,
                     has_side_effects=True,
-                    vmem_limit_bytes=63 * 2**20,
+                    vmem_limit_bytes=28 * 2**20,
                 ),
                 cost_estimate=estimate(400),
             )(

time: 304 us -> 295 us (0.970)
  Pallas kernels: 218 us -> 208 us
  waiting for transfers between devices: 34.8 us -> 41.6 us
  local copies, waits for them, and re-layouts: 28 us -> 21.2 us
    dynamic_update_slice x12, local copies, waits for them, and re-layouts: 12.7 us -> 0.7 us  [collect(): lax.dynamic_update_slice(whole, piece, (0, start, part * part_width))]
    unnamed x40 -> x60, local copies, waits for them, and re-layouts: 5.13 us -> 13.2 us
    pallas_call x2, Pallas kernels: 54.4 us -> 46.9 us  [per_device(): pl.pallas_call(functools.partial(forward_kernel, count, part_heads, part...]
    ppermute x5, waiting for transfers between devices: 34.8 us -> 39.5 us  [send(): return lax.ppermute(piece, 'track', perm)]
  transfers between devices with their start and end apart: 11 -> 11, of which waited for: 2 -> 3; matrix products, arithmetic and copies ran while one was open for 9% -> 4% of each run, Pallas kernels for 64% -> 63%
where the time goes in v4:
time: 295 us; the launch traced here: 294 us
  Pallas kernels  208 us (71%)
  waiting for transfers between devices  41.6 us (14%)
  local copies, waits for them, and re-layouts  21.2 us (7%)
  starting transfers between devices  15.2 us (5%)
  other arithmetic  7.18 us (2%)
    pallas_call x2, Pallas kernels, per_device(): pl.pallas_call(functools.partial(backward_kernel, count, part_heads, part...  142 us
    pallas_call x2, Pallas kernels, per_device(): pl.pallas_call(functools.partial(forward_kernel, count, part_heads, part...  46.9 us
    ppermute x5, waiting for transfers between devices, send(): return lax.ppermute(piece, 'track', perm)  39.5 us
    pallas_call x2, Pallas kernels, per_device(): pl.pallas_call(functools.partial(cross_kernel, groups, part_heads, 1.0 /...  19 us
    unnamed x60, local copies, waits for them, and re-layouts  13.2 us
    ppermute x6, starting transfers between devices, returned(): lax.ppermute(piece, 'track', back_perms[s])  9.15 us
    ppermute x5, starting transfers between devices, send(): return lax.ppermute(piece, 'track', perm)  6.05 us
  transfers between devices with their start and end apart: 11, of which 3 were waited for; matrix products, arithmetic and copies ran while one was open for 4% of the time, Pallas kernels for 63%

profile of v4, /device:TPU:0, one launch (start us, length us, event | category | flops | bytes accessed | tf_op | source)
XLA Modules:
  0.0 294.2 jit_solution(11191914217778054858)
XLA Ops:
  3.0 1.2 maximum_maximum_fusion.col_ref
  4.2 1.6 copy-done.13
  5.8 1.6 copy-done.15
  7.4 1.6 copy-done.17
  9.0 21.5 %shard_map.128 = (bf16[8,128,512]{2,1,0:T(8,128)(2,1)S(1)}, bf16[8,128,512]{2,1,0:T(8,128)(2,1)S(1)}, bf16[32,128,128]{2,1,0:T(8,128)(2,1)S(1)}) custom-call(bf16[8,128,1024]{2,1,0:T(8,128)(2,1)S(1)} %copy-done.13, bf16[8,128,1024]{2,1,0:T(8,128)(2,1)S(1)} %copy-done.15, bf16[8,128,1024]{2,1,0:T(8,128)(2,1)S(1)} %copy-done.17, ...), custom_call_target="tpu_custom_call" | custom-call | flops 53687091200 | bytes 8388608 | tf_op jit(solution)/shard_map/pallas_call | solution.py:372
  30.5 1.0 constant_dynamic-slice_fusion.1
  31.5 2.5 collective-permute-start.3
  34.3 1.1 constant_dynamic-slice_fusion.2
  36.3 1.1 constant_dynamic-slice_fusion.4
  37.4 1.2 collective-permute-start
  38.6 1.1 constant_dynamic-slice_fusion.3
  40.5 25.5 %shard_map.131 = (bf16[8,128,512]{2,1,0:T(8,128)(2,1)S(1)}, bf16[8,128,512]{2,1,0:T(8,128)(2,1)S(1)}, bf16[32,128,128]{2,1,0:T(8,128)(2,1)S(1)}) custom-call(bf16[8,128,1024]{2,1,0:T(8,128)(2,1)S(1)} %copy-done.13, bf16[8,128,1024]{2,1,0:T(8,128)(2,1)S(1)} %copy-done.15, bf16[8,128,1024]{2,1,0:T(8,128)(2,1)S(1)} %copy-done.17, ...), custom_call_target="tpu_custom_call" | custom-call | flops 53687091200 | bytes 8388608 | tf_op jit(solution)/shard_map/pallas_call | solution.py:372
  66.0 1.0 copy-done.25
  67.0 0.9 constant_dynamic-slice_fusion
  68.1 1.0 copy-done.9
  70.7 17.1 %collective-permute-done.refs_1_ = bf16[8,64,1024]{2,1,0:T(8,128)(2,1)} collective-permute-done((bf16[8,64,1024]{2,1,0:T(8,128)(2,1)}, bf16[8,64,1024]{2,1,0:T(8,128)(2,1)}, u32[]{:S(2)}, u32[]{:S(2)}) %collective-permute-start) | collective-permute-done | bytes 1048608 | tf_op jit(solution)/shard_map/ppermute | solution.py:330
  87.7 22.5 %collective-permute-done.1.refs_3_ = bf16[8,64,1024]{2,1,0:T(8,128)(2,1)} collective-permute-done((bf16[8,64,1024]{2,1,0:T(8,128)(2,1)}, bf16[8,64,1024]{2,1,0:T(8,128)(2,1)}, u32[]{:S(2)}, u32[]{:S(2)}) %collective-permute-start.1) | collective-permute-done | bytes 1048608 | tf_op jit(solution)/shard_map/ppermute | solution.py:330
  110.2 1.6 copy-done.2
  111.8 1.6 copy-done.5
  113.4 1.2 copy-done.8
  114.6 9.5 %shard_map.129 = (bf16[8,64,512]{2,1,0:T(8,128)(2,1)S(1)}, bf16[8,64,512]{2,1,0:T(8,128)(2,1)S(1)}, bf16[8,64,512]{2,1,0:T(8,128)(2,1)S(1)}, bf16[8,64,512]{2,1,...) custom-call(s32[1]{0:T(128)} %bitcast.4.own_ref, ...), custom_call_target="tpu_custom_call" | custom-call | flops 13421772800 | bytes 8388608 | tf_op jit(solution)/shard_map/pallas_call | solution.py:430
  124.2 2.6 collective-permute-start.9
  126.8 9.5 %shard_map.132 = (bf16[8,64,512]{2,1,0:T(8,128)(2,1)S(1)}, bf16[8,64,512]{2,1,0:T(8,128)(2,1)S(1)}, bf16[8,64,512]{2,1,0:T(8,128)(2,1)S(1)}, bf16[8,64,512]{2,1,...) custom-call(s32[1]{0:T(128)} %bitcast.4.own_ref, ...), custom_call_target="tpu_custom_call" | custom-call | flops 13421772800 | bytes 8388608 | tf_op jit(solution)/shard_map/pallas_call | solution.py:430
  136.3 2.0 collective-permute-start.10
  138.4 1.9 collective-permute-start.8
  141.4 2.1 collective-permute-done.4
  143.5 2.5 collective-permute-start.6
  146.1 99.6 %shard_map.130 = (bf16[8,128,512]{2,1,0:T(8,128)(2,1)S(1)}, bf16[8,128,512]{2,1,0:T(8,128)(2,1)S(1)}, bf16[8,128,512]{2,1,0:T(8,128)(2,1)S(1)}) custom-call(bf16[8,128,1024]{2,1,0:T(8,128)(2,1)S(1)} %copy-done.14, bf16[8,128,1024]{2,1,0:T(8,128)(2,1)S(1)} %copy-done.16, bf16[8,128,1024]{2,1,0:T(8,128)(2,1)S(1)} %copy-done.18, ...), custom_call_target="tpu_custom_call" | custom-call | flops 53687091200 | bytes 8388608 | tf_op jit(solution)/shard_map/pallas_call | solution.py:461
  245.7 42.1 %shard_map.133 = (bf16[8,128,512]{2,1,0:T(8,128)(2,1)S(1)}, bf16[8,128,512]{2,1,0:T(8,128)(2,1)S(1)}, bf16[8,128,512]{2,1,0:T(8,128)(2,1)S(1)}) custom-call(bf16[8,128,1024]{2,1,0:T(8,128)(2,1)S(1)} %copy-done.14, bf16[8,128,1024]{2,1,0:T(8,128)(2,1)S(1)} %copy-done.16, bf16[8,128,1024]{2,1,0:T(8,128)(2,1)S(1)} %copy-done.18, ...), custom_call_target="tpu_custom_call" | custom-call | flops 53687091200 | bytes 8388608 | tf_op jit(solution)/shard_map/pallas_call | solution.py:461
  288.2 1.8 pad_maximum_fusion.2
  290.2 2.6 pad_maximum_fusion
  292.9 1.3 copy-done.28
  (100 shorter events, 7.9 us)
Async XLA Ops:
  0.6 3.6 %copy-start.11 = (bf16[8,8,128,128]{3,2,1,0:T(8,128)(2,1)S(1)}, bf16[8,8,128,128]{3,2,1,0:T(8,128)(2,1)}, u32[]{:S(2)}) copy-start(bf16[8,8,128,128]{3,2,1,0:T(8,128)(2,1)} %init_ref.3) | copy-start | bytes 6291460
  4.2 1.6 copy-start.13
  9.0 25.1 %copy-start.29 = (bf16[8,128,1024]{2,1,0:T(8,128)(2,1)S(1)}, bf16[8,128,1024]{2,1,0:T(8,128)(2,1)}, u32[]{:S(2)}) copy-start(bf16[8,128,1024]{2,1,0:T(8,128)(2,1)} %param.17) | copy-start | bytes 6291460
  30.5 3.8 %copy-start.7 = (bf16[8,128,512]{2,1,0:T(8,128)(2,1)}, bf16[8,128,512]{2,1,0:T(8,128)(2,1)S(1)}, u32[]{:S(2)}) copy-start(bf16[8,128,512]{2,1,0:T(8,128)(2,1)S(1)} %get-tuple-element.30.refs_6_) | copy-start | bytes 3145732
  30.5 3.8 %copy-start.19 = (bf16[8,128,512]{2,1,0:T(8,128)(2,1)}, bf16[8,128,512]{2,1,0:T(8,128)(2,1)S(1)}, u32[]{:S(2)}) copy-start(bf16[8,128,512]{2,1,0:T(8,128)(2,1)S(1)} %get-tuple-element.29.out_ref) | copy-start | bytes 3145732
  30.5 3.8 %copy-start.21 = (bf16[32,128,128]{2,1,0:T(8,128)(2,1)}, bf16[32,128,128]{2,1,0:T(8,128)(2,1)S(1)}, u32[]{:S(2)}) copy-start(bf16[32,128,128]{2,1,0:T(8,128)(2,1)S(1)} %get-tuple-element.33.state_ref) | copy-start | bytes 3145732
  31.5 39.2 %collective-permute-start.3 = (bf16[8,64,512]{2,1,0:T(8,128)(2,1)}, bf16[8,64,512]{2,1,0:T(8,128)(2,1)S(1)}, u32[]{:S(2)}, u32[]{:S(2)}) collective-permute-start(bf16[8,64,512]{2,1,0:T(8,128)(2,1)} %constant_dynamic-slice_fusion.1), channel_id=1, source_target_pairs={{0,16},{16,0},{1,17},{17,1},{2,18},{18,2},{3,19},{19,3},{4,20},{20... | collective-permute-start | bytes 1572872 | tf_op jit(solution)/shard_map/ppermute | solution.py:330
  34.3 2.0 copy-start.1
  34.3 4.2 %copy-start.4 = (bf16[8,128,1024]{2,1,0:T(8,128)(2,1)S(1)}, bf16[8,128,1024]{2,1,0:T(8,128)(2,1)}, u32[]{:S(2)}) copy-start(bf16[8,128,1024]{2,1,0:T(8,128)(2,1)} %refs_2_.3) | copy-start | bytes 6291460
  35.4 5.1 %copy-start.12 = (bf16[8,8,128,128]{3,2,1,0:T(8,128)(2,1)S(1)}, bf16[8,8,128,128]{3,2,1,0:T(8,128)(2,1)}, u32[]{:S(2)}) copy-start(bf16[8,8,128,128]{3,2,1,0:T(8,128)(2,1)} %init_ref.3) | copy-start | bytes 6291460
  35.4 35.2 %collective-permute-start.2 = (bf16[8,64,1024]{2,1,0:T(8,128)(2,1)}, bf16[8,64,1024]{2,1,0:T(8,128)(2,1)}, u32[]{:S(2)}, u32[]{:S(2)}) collective-permute-start(bf16[8,64,1024]{2,1,0:T(8,128)(2,1)} %constant_dynamic-slice_fusion.2), channel_id=1, source_target_pairs={{0,16},{16,0},{1,17},{17,1},{2,18},{18,2},{3,19},{19,3},{4,20},{20... | collective-permute-start | bytes 3145736 | tf_op jit(solution)/shard_map/ppermute | solution.py:330
  37.4 50.4 %collective-permute-start = (bf16[8,64,1024]{2,1,0:T(8,128)(2,1)}, bf16[8,64,1024]{2,1,0:T(8,128)(2,1)}, u32[]{:S(2)}, u32[]{:S(2)}) collective-permute-start(bf16[8,64,1024]{2,1,0:T(8,128)(2,1)} %constant_dynamic-slice_fusion.4), channel_id=1, source_target_pairs={{0,16},{16,0},{1,17},{17,1},{2,18},{18,2},{3,19},{19,3},{4,20},{20... | collective-permute-start | bytes 3145736 | tf_op jit(solution)/shard_map/ppermute | solution.py:330
  39.6 70.6 %collective-permute-start.1 = (bf16[8,64,1024]{2,1,0:T(8,128)(2,1)}, bf16[8,64,1024]{2,1,0:T(8,128)(2,1)}, u32[]{:S(2)}, u32[]{:S(2)}) collective-permute-start(bf16[8,64,1024]{2,1,0:T(8,128)(2,1)} %constant_dynamic-slice_fusion.3), channel_id=1, source_target_pairs={{0,16},{16,0},{1,17},{17,1},{2,18},{18,2},{3,19},{19,3},{4,20},{20... | collective-permute-start | bytes 3145736 | tf_op jit(solution)/shard_map/ppermute | solution.py:330
  69.1 57.7 %collective-permute-start.5 = (bf16[8,64,512]{2,1,0:T(8,128)(2,1)}, bf16[8,64,512]{2,1,0:T(8,128)(2,1)}, u32[]{:S(2)}, u32[]{:S(2)}) collective-permute-start(bf16[8,64,512]{2,1,0:T(8,128)(2,1)} %constant_dynamic-slice_fusion), channel_id=1, source_target_pairs={{0,16},{16,0},{1,17},{17,1},{2,18},{18,2},{3,19},{19,3},{4,20},{20... | collective-permute-start | bytes 1572872 | tf_op jit(solution)/shard_map/ppermute | solution.py:330
  110.2 1.6 copy-start.2
  114.6 12.2 %copy-start.3 = (bf16[8,128,1024]{2,1,0:T(8,128)(2,1)S(1)}, bf16[8,128,1024]{2,1,0:T(8,128)(2,1)}, u32[]{:S(2)}) copy-start(bf16[8,128,1024]{2,1,0:T(8,128)(2,1)} %refs_0_.3) | copy-start | bytes 6291460
  114.6 12.2 %copy-start.6 = (bf16[8,128,1024]{2,1,0:T(8,128)(2,1)S(1)}, bf16[8,128,1024]{2,1,0:T(8,128)(2,1)}, u32[]{:S(2)}) copy-start(bf16[8,128,1024]{2,1,0:T(8,128)(2,1)} %refs_2_.3) | copy-start | bytes 6291460
  114.6 12.2 %copy-start.10 = (bf16[8,128,512]{2,1,0:T(8,128)(2,1)S(1)}, bf16[8,128,512]{2,1,0:T(8,128)(2,1)}, u32[]{:S(2)}) copy-start(bf16[8,128,512]{2,1,0:T(8,128)(2,1)} %copy-done.9) | copy-start | bytes 3145732
  124.2 163.6 %collective-permute-start.9 = (bf16[8,64,512]{2,1,0:T(8,128)(2,1)S(1)}, bf16[8,64,512]{2,1,0:T(8,128)(2,1)S(1)}, u32[]{:S(2)}, u32[]{:S(2)}) collective-permute-start(bf16[8,64,512]{2,1,0:T(8,128)(2,1)S(1)} %get-tuple-element.50), channel_id=1, source_target_pairs={{0,16},{16,0},{1,17},{17,1},{2,18},{18,2},{3,19},{19,3},{4,20},{20... | collective-permute-start | bytes 1572872 | tf_op jit(solution)/shard_map/ppermute | solution.py:409
  126.7 16.7 %collective-permute-start.4 = (bf16[8,64,512]{2,1,0:T(8,128)(2,1)S(1)}, bf16[8,64,512]{2,1,0:T(8,128)(2,1)S(1)}, u32[]{:S(2)}, u32[]{:S(2)}) collective-permute-start(bf16[8,64,512]{2,1,0:T(8,128)(2,1)S(1)} %get-tuple-element.32), channel_id=1, source_target_pairs={{0,16},{16,0},{1,17},{17,1},{2,18},{18,2},{3,19},{19,3},{4,20},{20... | collective-permute-start | bytes 1572872 | tf_op jit(solution)/shard_map/ppermute | solution.py:409
  136.3 151.8 %collective-permute-start.10 = (bf16[8,64,512]{2,1,0:T(8,128)(2,1)S(1)}, bf16[8,64,512]{2,1,0:T(8,128)(2,1)S(1)}, u32[]{:S(2)}, u32[]{:S(2)}) collective-permute-start(bf16[8,64,512]{2,1,0:T(8,128)(2,1)S(1)} %get-tuple-element.52), channel_id=1, source_target_pairs={{0,16},{16,0},{1,17},{17,1},{2,18},{18,2},{3,19},{19,3},{4,20},{20... | collective-permute-start | bytes 1572872 | tf_op jit(solution)/shard_map/ppermute | solution.py:409
  138.3 149.6 %collective-permute-start.7 = (bf16[8,64,512]{2,1,0:T(8,128)(2,1)S(1)}, bf16[8,64,512]{2,1,0:T(8,128)(2,1)S(1)}, u32[]{:S(2)}, u32[]{:S(2)}) collective-permute-start(bf16[8,64,512]{2,1,0:T(8,128)(2,1)S(1)} %get-tuple-element.46), channel_id=1, source_target_pairs={{0,16},{16,0},{1,17},{17,1},{2,18},{18,2},{3,19},{19,3},{4,20},{20... | collective-permute-start | bytes 1572872 | tf_op jit(solution)/shard_map/ppermute | solution.py:409
  138.4 154.4 %collective-permute-start.8 = (bf16[8,64,512]{2,1,0:T(8,128)(2,1)S(1)}, bf16[8,64,512]{2,1,0:T(8,128)(2,1)S(1)}, u32[]{:S(2)}, u32[]{:S(2)}) collective-permute-start(bf16[8,64,512]{2,1,0:T(8,128)(2,1)S(1)} %get-tuple-element.48), channel_id=1, source_target_pairs={{0,16},{16,0},{1,17},{17,1},{2,18},{18,2},{3,19},{19,3},{4,20},{20... | collective-permute-start | bytes 1572872 | tf_op jit(solution)/shard_map/ppermute | solution.py:409
  140.7 5.3 %copy-start.20 = (bf16[8,128,512]{2,1,0:T(8,128)(2,1)S(1)}, bf16[8,128,512]{2,1,0:T(8,128)(2,1)}, u32[]{:S(2)}) copy-start(bf16[8,128,512]{2,1,0:T(8,128)(2,1)} %copy-done.19) | copy-start | bytes 3145732
  140.7 5.3 %copy-start.22 = (bf16[32,128,128]{2,1,0:T(8,128)(2,1)S(1)}, bf16[32,128,128]{2,1,0:T(8,128)(2,1)}, u32[]{:S(2)}) copy-start(bf16[32,128,128]{2,1,0:T(8,128)(2,1)} %copy-done.21) | copy-start | bytes 3145732
  141.0 5.1 %copy-start.18 = (bf16[8,128,1024]{2,1,0:T(8,128)(2,1)S(1)}, bf16[8,128,1024]{2,1,0:T(8,128)(2,1)}, u32[]{:S(2)}) copy-start(bf16[8,128,1024]{2,1,0:T(8,128)(2,1)} %v_ref.7) | copy-start | bytes 6291460
  141.2 4.9 %copy-start.14 = (bf16[8,128,1024]{2,1,0:T(8,128)(2,1)S(1)}, bf16[8,128,1024]{2,1,0:T(8,128)(2,1)}, u32[]{:S(2)}) copy-start(bf16[8,128,1024]{2,1,0:T(8,128)(2,1)} %q_ref.7) | copy-start | bytes 6291460
  141.2 4.9 %copy-start.16 = (bf16[8,128,1024]{2,1,0:T(8,128)(2,1)S(1)}, bf16[8,128,1024]{2,1,0:T(8,128)(2,1)}, u32[]{:S(2)}) copy-start(bf16[8,128,1024]{2,1,0:T(8,128)(2,1)} %k_ref.7) | copy-start | bytes 6291460
  143.5 102.2 %collective-permute-start.6 = (bf16[8,64,512]{2,1,0:T(8,128)(2,1)S(1)}, bf16[8,64,512]{2,1,0:T(8,128)(2,1)S(1)}, u32[]{:S(2)}, u32[]{:S(2)}) collective-permute-start(bf16[8,64,512]{2,1,0:T(8,128)(2,1)S(1)} %get-tuple-element.38), channel_id=1, source_target_pairs={{0,16},{16,0},{1,17},{17,1},{2,18},{18,2},{3,19},{19,3},{4,20},{20... | collective-permute-start | bytes 1572872 | tf_op jit(solution)/shard_map/ppermute | solution.py:409
  146.1 99.7 %copy-start.24 = (bf16[8,128,512]{2,1,0:T(8,128)(2,1)S(1)}, bf16[8,128,512]{2,1,0:T(8,128)(2,1)}, u32[]{:S(2)}) copy-start(bf16[8,128,512]{2,1,0:T(8,128)(2,1)} %copy-done.23) | copy-start | bytes 3145732
  146.1 99.7 %copy-start.26 = (bf16[32,128,128]{2,1,0:T(8,128)(2,1)S(1)}, bf16[32,128,128]{2,1,0:T(8,128)(2,1)}, u32[]{:S(2)}) copy-start(bf16[32,128,128]{2,1,0:T(8,128)(2,1)} %copy-done.25) | copy-start | bytes 3145732
  288.2 2.0 copy-start.27
  (9 other events, 11.4 us)
